TPU v7x, 128 devices: a whole 4x4x4 slice. The times are simulated.
128 devices in a mesh: gx: 8 (over y, core), gy: 16 (over z, x).
Axes of the slice: x: 4, y: 4, z: 4, core: 2. Of those that a mesh axis runs over, the one named last changes fastest.
Arguments:
- thermal_anomaly: float32 [32, 256, 2048], P(None, 'gx', 'gy'), may hold values from -6 to 6
- ambient_diffusion: bfloat16 [256, 2048], P('gx', 'gy'), may hold values from 0.019897461 to 0.25
- solar_light: bfloat16 [256, 2048], P('gx', 'gy'), may hold values from 0.5 to 4
- sea_tile_flags: int32 [8, 16, 64], P('gx', 'gy'), may hold values 0 or 1
- flooded_layer_tally: int32 [8, 16, 64], P('gx', 'gy'), may hold values from 1 to 32
- tile_holder_rank: int32 [8, 16, 64, 1], P('gx', 'gy'), may hold values from 0 to 15; in each aligned block of 64 rows (0 to 63, 64 to 127, ..., all dimensions but the last counted through in order) at most 8 rows name the same one
- solute_amounts: float32 [8, 16, 128, 8, 2048], P('gx', 'gy'), may hold values from 0.09 to 11
- reaction_rates: float32 [8, 8], replicated, may hold values from -0.2 to 0.5
Outputs:
- thermal_final: float32 [32, 256, 2048], P(None, 'gx', 'gy')
- solute_final: float32 [8, 16, 128, 8, 2048], P('gx', 'gy')
Inputs may be any that keep to these rules, and one draw needn't show every extreme that they name: `tile_holder_rank`: among the 64 blocks of one device, at most 8 name the same owner, a bound that some block reaches of them.
All inputs are finite; a program needn't handle non-finite values. No bound on the sum of `sea_tile_flags` on one device may be relied on, other than what follows from the above.
Results may differ from a plain program's by a relative error of at most 0.0003.
Values may be sent and summed in bfloat16 or wider, within the bound.
A program may use at most 128 MiB of HBM per device.

v0:
```python
import jax
import jax.numpy as jnp
from jax import lax
from jax.sharding import Mesh
from jax.sharding import PartitionSpec as P

GX_GY = ("gx_0", "gx_1", "gy_0", "gy_1")
GX = ("gx_0", "gx_1")
GY = ("gy_0", "gy_1")


NU_COEF = 0.2
STEP_DT = 0.05
ATTEN_WATER = 0.06
ATTEN_CHL = 0.05
WARMING_SCALE = 0.5
GROWTH_TEMP = 0.063


def with_halo(shard, sides, width):
    edges = {}
    for axis, dim in sides:
        count, length = (lax.axis_size(axis), shard.shape[dim])
        up = [(i, (i + 1) % count) for i in range(count - 1)]
        last = lax.slice_in_dim(shard, length - width, length, axis=dim)
        initial = lax.slice_in_dim(shard, 0, width, axis=dim)
        edges[dim] = (
            lax.ppermute(last, axis, up),
            lax.ppermute(initial, axis, [(b, a) for a, b in up]),
        )
    done = []
    for _, dim in sides:
        low, high = edges[dim]
        around = [(width, width) if d in done else (0, 0) for d in range(shard.ndim)]
        shard = jnp.concatenate([jnp.pad(low, around), shard, jnp.pad(high, around)], axis=dim)
        done.append(dim)
    return shard


def by_axis(shard, axes):
    for axis in axes:
        shard = lax.psum(shard, axis)
    return shard


def masked_step(field, within_layer):
    center = field[:, 1:-1, 1:-1]
    span_east = center.shape[1]
    span_north = center.shape[2]
    total = jnp.zeros_like(center)
    for first, second in ((0, 1), (2, 1), (1, 0), (1, 2)):
        near = field[:, first : first + span_east, second : second + span_north]
        total = total + within_layer[:, first : first + span_east, second : second + span_north] * (
            near - center
        )
    return center + NU_COEF * within_layer[:, 1:-1, 1:-1] * total


def level_below(values):
    return jnp.concatenate([values[..., 64:], values[..., -64:]], axis=-1)


def level_above_zero(values):
    return jnp.concatenate([jnp.zeros_like(values[..., :64]), values[..., :-64]], axis=-1)


def level_prefix(values, layer_tally):
    running = values
    reach = 1
    while reach < layer_tally:
        moved = jnp.concatenate(
            [jnp.zeros_like(running[..., : 64 * reach]), running[..., : -64 * reach]], axis=-1
        )
        running = running + moved
        reach = reach * 2
    return running


def spread_levels(column_values, layer_tally):
    return jnp.tile(column_values, (1, layer_tally))


def flat_mixer(temp_flat, kbg_flat):
    return (kbg_flat * (1.0 + 0.5 * jnp.tanh(temp_flat - level_below(temp_flat)))).astype(
        jnp.bfloat16
    )


def flat_validity(tile_amount, flat_width):
    levels = lax.broadcasted_iota(jnp.int32, (1, flat_width), 1) // 64
    valid = (levels < tile_amount[:, None]).astype(jnp.float32)
    active = (levels + 1 < tile_amount[:, None]).astype(jnp.float32)
    return (valid, active)


def totals(amounts_on_chip, valid):
    return jnp.sum(amounts_on_chip * valid[:, None], axis=(0, 2))


def column_step(
    temp_flat, kappa_flat, surface, valid, active, amounts_on_chip, reaction_rates, layer_tally
):
    atten = ATTEN_WATER + ATTEN_CHL * amounts_on_chip[:, 0]
    cumul = level_prefix(atten, layer_tally)
    top = surface * jnp.exp(-(cumul - atten))
    bottom = surface * jnp.exp(-cumul)
    heat = (valid * (top - bottom)).astype(jnp.bfloat16)
    growth = jnp.exp(GROWTH_TEMP * temp_flat.astype(jnp.float32)) * top / (top + 1.0)
    mixed = jnp.einsum(
        "rs,nsf->nrf", reaction_rates, amounts_on_chip, precision=lax.Precision.HIGHEST
    )
    flux = (kappa_flat.astype(jnp.float32) * active)[:, None] * (
        level_below(amounts_on_chip) - amounts_on_chip
    )
    new = amounts_on_chip + valid[:, None] * STEP_DT * (
        flux - level_above_zero(flux) + growth[:, None] * mixed
    )
    return (new, heat)


def plane_blocks(field, blocks_x, blocks_y):
    return (
        field.reshape(blocks_x, 8, blocks_y, 8)
        .transpose(0, 2, 1, 3)
        .reshape(blocks_x * blocks_y, 64)
    )


def on_device(
    thermal_anomaly,
    ambient_diffusion,
    solar_light,
    sea_tile_flags,
    flooded_layer_tally,
    tile_holder_rank,
    solute_amounts,
    reaction_rates,
):
    layer_tally = thermal_anomaly.shape[0]
    span_east = thermal_anomaly.shape[1]
    span_north = thermal_anomaly.shape[2]
    blocks_x = span_east // 8
    blocks_y = span_north // 8
    tile_summation = blocks_x * blocks_y
    flat_width = layer_tally * 64
    depth_block = (sea_tile_flags * flooded_layer_tally).reshape(tile_summation)
    cell_count = jnp.repeat(
        jnp.repeat(depth_block.reshape(blocks_x, blocks_y), 8, axis=0), 8, axis=1
    )
    level_idx = lax.broadcasted_iota(jnp.int32, (layer_tally, 1, 1), 0)
    joined = jnp.concatenate([thermal_anomaly, cell_count[None].astype(jnp.float32)], axis=0)
    padded = with_halo(joined, ((GX, 1), (GY, 2)), 1)
    inside_pad = (level_idx.astype(jnp.float32) < padded[layer_tally : layer_tally + 1]).astype(
        jnp.float32
    )
    advanced_verticals = masked_step(padded[:layer_tally], inside_pad)
    dispatched = advanced_verticals.astype(jnp.bfloat16)
    thermal_tiles = (
        dispatched.reshape(layer_tally, blocks_x, 8, blocks_y, 8)
        .transpose(1, 3, 0, 2, 4)
        .reshape(tile_summation, flat_width)
    )
    ambient_diffusion_tiles = plane_blocks(ambient_diffusion, blocks_x, blocks_y)
    shortwave_blocks = plane_blocks(solar_light, blocks_x, blocks_y)
    diffusion_each_tile = flat_mixer(
        thermal_tiles.astype(jnp.float32),
        spread_levels(ambient_diffusion_tiles.astype(jnp.float32), layer_tally),
    )
    payload = jnp.concatenate([thermal_tiles, diffusion_each_tile, shortwave_blocks], axis=1)
    holder_chip = tile_holder_rank.reshape(tile_summation)
    order = jnp.arange(tile_summation, dtype=jnp.int32)
    same = (holder_chip[:, None] == holder_chip[None, :]) & (order[None, :] < order[:, None])
    rank = jnp.sum(same.astype(jnp.int32), axis=1)
    position_summation = solute_amounts.shape[2]
    device_groups = lax.axis_size(GY)
    slot_limit = position_summation // device_groups
    target_owner = holder_chip * slot_limit + rank
    selection_mask = (
        lax.broadcasted_iota(jnp.int32, (position_summation, tile_summation), 0)
        == target_owner[None, :]
    )
    select_b = selection_mask.astype(jnp.bfloat16)
    packed = jnp.einsum("sb,bf->sf", select_b, payload, preferred_element_type=jnp.float32).astype(
        jnp.bfloat16
    )
    packed_count = jnp.sum(selection_mask.astype(jnp.int32) * depth_block[None, :], axis=1)
    arrived_tiles, received_count = (
        lax.all_to_all(
            packed.reshape(device_groups, slot_limit, packed.shape[1]),
            GY,
            split_axis=0,
            concat_axis=0,
            tiled=True,
        ),
        lax.all_to_all(
            packed_count.reshape(device_groups, slot_limit),
            GY,
            split_axis=0,
            concat_axis=0,
            tiled=True,
        ),
    )
    arrived_tiles = arrived_tiles.reshape(position_summation, arrived_tiles.shape[2])
    tile_amount = received_count.reshape(position_summation)
    thermal_at_position = arrived_tiles[:, :flat_width]
    diffusion_at_position = arrived_tiles[:, flat_width : 2 * flat_width]
    solar_at_position = arrived_tiles[:, 2 * flat_width :]
    surface = spread_levels(solar_at_position.astype(jnp.float32), layer_tally)
    amounts_on_chip = solute_amounts.reshape(
        position_summation, solute_amounts.shape[3], flat_width
    )
    valid, active = flat_validity(tile_amount, flat_width)
    old_local = totals(amounts_on_chip, valid)
    cells_local = jnp.sum(valid)
    new, heat = column_step(
        thermal_at_position,
        diffusion_at_position,
        surface,
        valid,
        active,
        amounts_on_chip,
        reaction_rates,
        layer_tally,
    )
    old_total, cells, new_total = (
        by_axis(old_local, GX_GY),
        by_axis(cells_local, GX_GY),
        by_axis(totals(new, valid), GX_GY),
    )
    shift = (old_total - new_total) / jnp.maximum(cells, 1.0)
    solute_final = jnp.where(
        valid[:, None] > 0, new + shift[None, :, None], amounts_on_chip
    ).reshape(solute_amounts.shape)
    returned_blocks = lax.all_to_all(
        heat.reshape(device_groups, slot_limit, flat_width),
        GY,
        split_axis=0,
        concat_axis=0,
        tiled=True,
    )
    returned_blocks = returned_blocks.reshape(position_summation, flat_width)
    heat_blocks = jnp.einsum(
        "sb,sf->bf", select_b, returned_blocks, preferred_element_type=jnp.float32
    )
    warming_each_site = (
        heat_blocks.reshape(blocks_x, blocks_y, layer_tally, 8, 8)
        .transpose(2, 0, 3, 1, 4)
        .reshape(layer_tally, span_east, span_north)
    )
    thermal_final = advanced_verticals + WARMING_SCALE * warming_each_site
    return (thermal_final, solute_final)


def solution(mesh):
    finer = Mesh(mesh.devices.reshape(4, 2, 4, 4), ("gx_0", "gx_1", "gy_0", "gy_1"))
    in_specs = (
        P(None, GX, GY),
        P(GX, GY),
        P(GX, GY),
        P(GX, GY, None),
        P(GX, GY, None),
        P(GX, GY, None, None),
        P(GX, GY, None, None, None),
        P(),
    )
    out_specs = (P(None, GX, GY), P(GX, GY, None, None, None))
    return jax.shard_map(
        on_device, mesh=finer, in_specs=in_specs, out_specs=out_specs, check_vma=False
    )
```

profile of v0, /device:TPU:0, one launch (start us, length us, event | category | flops | bytes accessed | tf_op | source)
XLA Modules:
  0.0 178.2 jit_solution(17803232174242923997)
XLA Ops:
  0.6 0.7 convert_reduce_fusion.1
  1.6 1.5 fusion.17
  3.5 3.5 %collective-permute-start = (f32[33,32,1]{0,1,2:T(8,128)S(1)}, f32[33,32,1]{0,1,2:T(8,128)S(1)}, u32[]{:S(2)}, u32[]{:S(2)}) collective-permute-start(f32[33,32,1]{0,1,2:T(8,128)S(1)} %copy.106), channel_id=1, source_target_pairs={{0,1},{1,2},{2,3},{3,4},{4,5},{5,6},{6,7},{7,8},{8,9},{9,10},{10,1... | collective-permute-start | bytes 12680 | tf_op jit(solution)/shard_map/ppermute | solution.py:28
  7.4 1.3 collective-permute-start.3
  8.7 1.0 fusion.37
  9.7 1.5 collective-permute-start.1
  11.2 1.3 collective-permute-start.2
  12.5 0.7 multiply_bitcast_fusion.1
  13.2 0.9 convert_reduce_fusion
  14.1 0.7 multiply_add_fusion
  14.8 0.7 all_to_all.12
  15.5 8.9 %all-to-all-start = ((s32[16,1,8]{2,1,0:T(1,128)}), s32[16,1,8]{2,1,0:T(1,128)S(1)}, u32[]{:S(2)}, u32[]{:S(2)}) async-start(s32[16,1,8]{2,1,0:T(1,128)} %bitcast.8), calls=%async_computation | async-start | bytes 16384 | tf_op jit(solution)/shard_map/all_to_all | solution.py:195
  24.4 4.8 %fusion.9 = f32[128,1,2048]{2,1,0:T(1,128)S(1)} fusion(f32[128,8,2048]{2,1,0:T(8,128)} %bitcast.77), kind=kLoop, calls=%fused_computation.21 | loop fusion | flops 524288 | bytes 2097152 | tf_op jit(solution)/shard_map/add | solution.py:103
  31.4 1.3 copy.107
  32.7 1.1 pad.13
  33.9 1.3 copy.109
  35.2 1.1 pad.14
  36.6 2.0 %fusion.45 = (bf16[32,32,128]{2,1,0:T(8,128)(2,1)}, f32[32,32,128]{2,1,0:T(8,128)}) fusion(f32[32,32,128]{2,1,0:T(8,128)S(1)} %copy-done.1, f32[33,34,1]{2,1,0:T(8,128)S(1)} %pad.14, f32[33,1,128]{2,1,0:T(1,128)S(1)} %collective-permute-done.2, f32[1,32,128]{2,1,0:T(8,128)S(1)} %copy.105, f32[33,1,128]{2,1,0:T(1,128)S(1)} %collective-permute-done.1, ...), kind=kLoop, calls=%fused_computation.108 | loop fusion | flops 3538944 | bytes 3991312 | tf_op jit(solution)/shard_map/convert_element_type | solution.py:157
  38.6 2.3 %copy.111 = bf16[32,32,128]{0,2,1:T(8,128)(2,1)} copy(bf16[32,32,128]{2,1,0:T(8,128)(2,1)} %get-tuple-element.20) | data formatting | bytes 524288 | tf_op jit(solution)/shard_map/convert_element_type | solution.py:157
  40.9 4.9 %copy.112 = bf16[4,16,32,8,8]{1,0,4,3,2:T(4,128)(2,1)S(1)} copy(bf16[4,16,32,8,8]{2,4,1,3,0:T(8,128)(2,1)} %bitcast.83) | data formatting | bytes 524288 | tf_op jit(solution)/shard_map/transpose | solution.py:160
  45.9 1.7 reshape.250
  47.7 1.2 slice.138
  48.9 0.7 slice.139
  49.6 1.3 fusion.14
  50.9 2.5 %convolution_convert_fusion = bf16[128,4160]{0,1:T(8,128)(2,1)} fusion(bf16[64,64]{0,1:T(8,128)(2,1)S(1)} %reshape.252, bf16[64,2048]{0,1:T(8,128)(2,1)S(1)} %fusion.14, bf16[64,2048]{0,1:T(8,128)(2,1)} %reshape.250, s32[64]{0:T(128)S(1)} %multiply_add_fusion), kind=kOutput, calls=%fused_computation.8 | convolution fusion | flops 70295552 | bytes 1597696 | tf_op jit(solution)/shard_map/sb,bf->sf/dot_general | solution.py:183
  53.5 2.4 %copy.115 = bf16[128,4160]{1,0:T(8,128)(2,1)} copy(bf16[128,4160]{0,1:T(8,128)(2,1)} %convolution_convert_fusion) | data formatting | bytes 2129920 | tf_op jit(solution)/shard_map/convert_element_type | solution.py:183
  55.8 7.3 %all-to-all-start.1 = ((bf16[16,8,4160]{2,1,0:T(8,128)(2,1)}), bf16[16,8,4160]{2,1,0:T(8,128)(2,1)}, u32[]{:S(2)}, u32[]{:S(2)}) async-start(bf16[16,8,4160]{2,1,0:T(8,128)(2,1)} %bitcast.82), calls=%async_computation.1 | async-start | bytes 2162688 | tf_op jit(solution)/shard_map/all_to_all | solution.py:188
  63.3 9.4 %slice.148 = f32[128,8,1984]{2,1,0:T(8,128)} slice(f32[128,8,2048]{2,1,0:T(8,128)} %bitcast.78), slice={[0:128], [0:8], [64:2048]} | slice | bytes 16252928 | tf_op jit(solution)/shard_map/slice | solution.py:60
  72.6 2.1 %slice.149 = f32[128,8,64]{2,1,0:T(8,128)} slice(f32[128,8,2048]{2,1,0:T(8,128)} %bitcast.79), slice={[0:128], [0:8], [1984:2048]} | slice | bytes 524288 | tf_op jit(solution)/shard_map/slice | solution.py:60
  74.7 0.9 slice.146
  76.1 0.6 reduce.7
  76.8 1.3 fusion.16
  78.1 2.9 %all-to-all-done.1 = bf16[16,8,4160]{2,1,0:T(8,128)(2,1)} async-done(((bf16[16,8,4160]{2,1,0:T(8,128)(2,1)}), bf16[16,8,4160]{2,1,0:T(8,128)(2,1)}, u32[]{:S(2)}, u32[]{:S(2)}) %all-to-all-start.1) | async-done | bytes 1064992 | tf_op jit(solution)/shard_map/all_to_all | solution.py:188
  81.0 0.8 slice.140
  82.0 1.4 copy.117
  83.3 4.9 %add_divide_fusion = (f32[128,2048]{1,0:T(8,128)S(1)}, bf16[16,8,2048]{2,1,0:T(8,128)(2,1)}, f32[128,2048]{1,0:T(8,128)}, f32[]{:T(128)}, f32[128,2048]{1,0:T(8,128)S(1)}) fusion(f32[128,2048]{1,0:T(8,128)} %copy.117, f32[128,2048]{1,0:T(8,128)} %copy-done.4, f32[128,1024]{1,0:T(8,128)} %slice.146, bf16[128,4160]{1,0:T(8,128)(2,1)} %bitcast.15, ...), kind=kLoop, calls=%fused_computation.29 | loop fusion | flops 5505023 | bytes 8405508 | tf_op jit(solution)/shard_map/div | solution.py:108
  88.3 4.6 %all-to-all-start.2 = ((bf16[16,8,2048]{2,1,0:T(8,128)(2,1)}), bf16[16,8,2048]{2,1,0:T(8,128)(2,1)S(1)}, u32[]{:S(2)}, u32[]{:S(2)}) async-start(bf16[16,8,2048]{2,1,0:T(8,128)(2,1)} %get-tuple-element.23), calls=%async_computation.2 | async-start | bytes 1048576 | tf_op jit(solution)/shard_map/all_to_all | solution.py:234
  92.9 8.0 %fusion = f32[128,8,2048]{2,1,0:T(8,128)S(1)} fusion(f32[128,8,64]{2,1,0:T(8,128)} %slice.149, f32[128,8,1984]{2,1,0:T(8,128)} %slice.148, f32[128,2048]{1,0:T(8,128)} %get-tuple-element.24, f32[1,1,128,8,2048]{4,3,2,1,0:T(8,128)} %param.14), kind=kLoop, calls=%fused_computation.1 | loop fusion | flops 6291456 | bytes 26214400 | tf_op jit(solution)/shard_map/mul | solution.py:112
  100.9 24.2 %multiply_reduce_fusion = (f32[8]{0:T(128)S(1)}, f32[8]{0:T(128)S(1)}, f32[128,8,2048]{2,1,0:T(8,128)}) fusion(f32[128,2048]{1,0:T(8,128)S(1)} %copy-done.5, f32[1,1,128,8,2048]{4,3,2,1,0:T(8,128)} %param.14, f32[8,8]{1,0:T(8,128)S(1)} %copy-done, f32[128,2048]{1,0:T(8,128)S(1)} %get-tuple-element.22, f32[128,8,2048]{2,1,0:T(8,128)S(1)} %fusion, ...), kind=kOutput, calls=%fused_computation.6 | convolution fusion | flops 220200944 | bytes 36438336 | tf_op jit(solution)/shard_map/rs,nsf->nrf/dot_general | solution.py:109
  125.1 13.9 %all-reduce.10 = (f32[8]{0:T(128)S(1)}, f32[8]{0:T(128)S(1)}, f32[]{:T(128)}) all-reduce(f32[8]{0:T(128)S(1)} %get-tuple-element.7, f32[8]{0:T(128)S(1)} %get-tuple-element.6, f32[]{:T(128)} %get-tuple-element.29), channel_id=1, replica_groups=mesh['gx_0'=4,'gx_1'=2,'gy_0'=4,'gy_1'=4] {'gx_0'}, use_global_device_ids=true, to_apply=%region_3.4 | all-reduce | flops 17 | bytes 136 | tf_op jit(solution)/shard_map/psum | solution.py:42
  139.0 3.1 %all-reduce.11 = (f32[8]{0:T(128)S(1)}, f32[8]{0:T(128)S(1)}, f32[]{:T(128)}) all-reduce(f32[8]{0:T(128)S(1)} %get-tuple-element.14, f32[8]{0:T(128)S(1)} %get-tuple-element.15, f32[]{:T(128)} %get-tuple-element.16), channel_id=1, replica_groups=mesh['gx_0'=4,'gx_1'=2,'gy_0'=4,'gy_1'=4] {'gx_1'}, use_global_device_ids=true, to_apply=%region_4.5 | all-reduce | flops 17 | bytes 136 | tf_op jit(solution)/shard_map/psum | solution.py:42
  142.1 11.5 %all-reduce.9 = (f32[8]{0:T(128)S(1)}, f32[8]{0:T(128)S(1)}, f32[]{:T(128)}) all-reduce(f32[8]{0:T(128)S(1)} %get-tuple-element.17, f32[8]{0:T(128)S(1)} %get-tuple-element.18, f32[]{:T(128)} %get-tuple-element.19), channel_id=1, replica_groups=mesh['gx_0'=4,'gx_1'=2,'gy_0'=4,'gy_1'=4] {'gy_0'}, use_global_device_ids=true, to_apply=%region_5.6 | all-reduce | flops 17 | bytes 136 | tf_op jit(solution)/shard_map/psum | solution.py:42
  153.6 11.0 %all-reduce.8 = (f32[8]{0:T(128)S(1)}, f32[8]{0:T(128)S(1)}, f32[]{:T(128)}) all-reduce(f32[8]{0:T(128)S(1)} %get-tuple-element.11, f32[8]{0:T(128)S(1)} %get-tuple-element.12, f32[]{:T(128)} %get-tuple-element.13), channel_id=1, replica_groups=mesh['gx_0'=4,'gx_1'=2,'gy_0'=4,'gy_1'=4] {'gy_1'}, use_global_device_ids=true, to_apply=%region_6.7 | all-reduce | flops 17 | bytes 136 | tf_op jit(solution)/shard_map/psum | solution.py:42
  165.2 9.3 %select_bitcast_fusion = f32[1,1,128,8,2048]{4,3,2,1,0:T(8,128)} fusion(f32[128,8,2048]{2,1,0:T(8,128)} %get-tuple-element.33, f32[8]{0:T(128)S(1)} %subtract_divide_fusion, pred[128,2048]{1,0:T(8,128)(4,1)S(1)} %get-tuple-element.31, f32[1,1,128,8,2048]{4,3,2,1,0:T(8,128)} %param.14), kind=kLoop, calls=%fused_computation.5 | loop fusion | flops 4194304 | bytes 25428000 | tf_op jit(solution)/shard_map/reshape | solution.py:233
  174.7 1.0 multiply_bitcast_fusion
  175.7 0.9 copy.121
  176.6 0.7 copy.122
  177.3 0.9 add.145
  (58 shorter events, 4.8 us)
Async XLA Ops:
  0.6 100.2 %copy-start = (f32[8,8]{1,0:T(8,128)S(1)}, f32[8,8]{1,0:T(8,128)}, u32[]{:S(2)}) copy-start(f32[8,8]{1,0:T(8,128)} %param.15) | copy-start | bytes 772
  3.5 27.9 %collective-permute-start = (f32[33,32,1]{0,1,2:T(8,128)S(1)}, f32[33,32,1]{0,1,2:T(8,128)S(1)}, u32[]{:S(2)}, u32[]{:S(2)}) collective-permute-start(f32[33,32,1]{0,1,2:T(8,128)S(1)} %copy.106), channel_id=1, source_target_pairs={{0,1},{1,2},{2,3},{3,4},{4,5},{5,6},{6,7},{7,8},{8,9},{9,10},{10,1... | collective-permute-start | bytes 12680 | tf_op jit(solution)/shard_map/ppermute | solution.py:28
  7.4 26.4 %collective-permute-start.3 = (f32[33,32,1]{0,1,2:T(8,128)S(1)}, f32[33,32,1]{0,1,2:T(8,128)S(1)}, u32[]{:S(2)}, u32[]{:S(2)}) collective-permute-start(f32[33,32,1]{0,1,2:T(8,128)S(1)} %copy.108), channel_id=1, source_target_pairs={{1,0},{2,1},{3,2},{4,3},{5,4},{6,5},{7,6},{8,7},{9,8},{10,9},{11,1... | collective-permute-start | bytes 12680 | tf_op jit(solution)/shard_map/ppermute | solution.py:29
  9.7 26.6 %collective-permute-start.1 = (f32[33,1,128]{2,1,0:T(1,128)S(1)}, f32[33,1,128]{2,1,0:T(1,128)S(1)}, u32[]{:S(2)}, u32[]{:S(2)}) collective-permute-start(f32[33,1,128]{2,1,0:T(1,128)S(1)} %get-tuple-element.27), channel_id=1, source_target_pairs={{0,16},{16,32},{32,48},{48,64},{64,80},{80,96},{96,112},{1,17},{17... | collective-permute-start | bytes 50696 | tf_op jit(solution)/shard_map/ppermute | solution.py:28
  11.2 25.2 %collective-permute-start.2 = (f32[33,1,128]{2,1,0:T(1,128)S(1)}, f32[33,1,128]{2,1,0:T(1,128)S(1)}, u32[]{:S(2)}, u32[]{:S(2)}) collective-permute-start(f32[33,1,128]{2,1,0:T(1,128)S(1)} %get-tuple-element.28), channel_id=1, source_target_pairs={{16,0},{32,16},{48,32},{64,48},{80,64},{96,80},{112,96},{17,1},{33... | collective-permute-start | bytes 50696 | tf_op jit(solution)/shard_map/ppermute | solution.py:29
  15.5 40.3 %all-to-all-start = ((s32[16,1,8]{2,1,0:T(1,128)}), s32[16,1,8]{2,1,0:T(1,128)S(1)}, u32[]{:S(2)}, u32[]{:S(2)}) async-start(s32[16,1,8]{2,1,0:T(1,128)} %bitcast.8), calls=%async_computation | async-start | bytes 16384 | tf_op jit(solution)/shard_map/all_to_all | solution.py:195
  24.4 6.1 %copy-start.7 = (bf16[32,128]{1,0:T(8,128)(2,1)S(1)}, bf16[32,128]{1,0:T(8,128)(2,1)}, u32[]{:S(2)}) copy-start(bf16[32,128]{1,0:T(8,128)(2,1)} %param.9) | copy-start | bytes 24580
  29.2 1.7 copy-start.8
  30.1 6.3 %copy-start.1 = (f32[32,32,128]{2,1,0:T(8,128)S(1)}, f32[32,32,128]{2,1,0:T(8,128)}, u32[]{:S(2)}) copy-start(f32[32,32,128]{2,1,0:T(8,128)} %param.8) | copy-start | bytes 1572868
  30.5 10.5 %copy-start.2 = (f32[128,2048]{1,0:T(8,128)}, f32[128,2048]{1,0:T(8,128)S(1)}, u32[]{:S(2)}) copy-start(f32[128,2048]{1,0:T(8,128)S(1)} %pad_add_fusion.2) | copy-start | bytes 3145732
  47.7 15.5 %copy-start.3 = (f32[128,2048]{1,0:T(8,128)S(1)}, f32[128,2048]{1,0:T(8,128)}, u32[]{:S(2)}) copy-start(f32[128,2048]{1,0:T(8,128)} %copy-done.2) | copy-start | bytes 3145732
  47.7 15.5 %slice-start = ((f32[128,2048]{1,0:T(8,128)}), f32[128,1536]{1,0:T(8,128)S(1)}, s32[]{:S(2)}) async-start(f32[128,2048]{1,0:T(8,128)} %copy-done.2), calls=%async_computation.3 | async-start | bytes 1572864 | tf_op jit(solution)/shard_map/slice | solution.py:72
  55.8 25.1 %all-to-all-start.1 = ((bf16[16,8,4160]{2,1,0:T(8,128)(2,1)}), bf16[16,8,4160]{2,1,0:T(8,128)(2,1)}, u32[]{:S(2)}, u32[]{:S(2)}) async-start(bf16[16,8,4160]{2,1,0:T(8,128)(2,1)} %bitcast.82), calls=%async_computation.1 | async-start | bytes 2162688 | tf_op jit(solution)/shard_map/all_to_all | solution.py:188
  63.2 11.5 %copy-start.4 = (f32[128,2048]{1,0:T(8,128)}, f32[128,2048]{1,0:T(8,128)S(1)}, u32[]{:S(2)}) copy-start(f32[128,2048]{1,0:T(8,128)S(1)} %pad_add_fusion.1) | copy-start | bytes 3145732
  88.3 86.2 %all-to-all-start.2 = ((bf16[16,8,2048]{2,1,0:T(8,128)(2,1)}), bf16[16,8,2048]{2,1,0:T(8,128)(2,1)S(1)}, u32[]{:S(2)}, u32[]{:S(2)}) async-start(bf16[16,8,2048]{2,1,0:T(8,128)(2,1)} %get-tuple-element.23), calls=%async_computation.2 | async-start | bytes 1048576 | tf_op jit(solution)/shard_map/all_to_all | solution.py:234
  92.9 8.0 %copy-start.5 = (f32[128,2048]{1,0:T(8,128)S(1)}, f32[128,2048]{1,0:T(8,128)}, u32[]{:S(2)}) copy-start(f32[128,2048]{1,0:T(8,128)} %get-tuple-element.32) | copy-start | bytes 3145732
  174.4 2.9 %copy-start.6 = (f32[32,32,128]{2,1,0:T(8,128)S(1)}, f32[32,32,128]{2,1,0:T(8,128)}, u32[]{:S(2)}) copy-start(f32[32,32,128]{2,1,0:T(8,128)} %get-tuple-element.21) | copy-start | bytes 1572868
where the time goes:
time: 179 us; the launch traced here: 178 us
  other arithmetic  39.7 us (22%)
  blocking collectives  39.5 us (22%)
  local copies, waits for them, and re-layouts  38.5 us (22%)
  starting transfers between devices  28.2 us (16%)
  matrix products  27.8 us (16%)
  waiting for transfers between devices  2.92 us (2%)
    psum x4, blocking collectives, by_axis(): shard = lax.psum(shard, axis)  39.5 us
    dot_general x1, matrix products, column_step(): jnp.einsum('rs,nsf->nrf', reaction_rates, amounts_on_chip, precision=lax....  24.2 us
    slice x4, local copies, waits for them, and re-layouts, level_below(): return jnp.concatenate([values[..., 64:], values[..., -64:]], axis=-1)  13.4 us
    reshape x1, other arithmetic, on_device(): solute_final = jnp.where(valid[:, None] > 0, new + shift[None, :, None],...  9.28 us
    all_to_all x1, starting transfers between devices, on_device(): lax.all_to_all(packed_count.reshape(device_groups, slot_limit), GY, split...  8.86 us
    mul x1, other arithmetic, column_step(): (kappa_flat.astype(jnp.float32) * active)[:, None]  7.96 us
    all_to_all x1, starting transfers between devices, on_device(): lax.all_to_all(packed.reshape(device_groups, slot_limit, packed.shape[1])...  7.27 us
    transpose x1, local copies, waits for them, and re-layouts, on_device(): thermal_tiles = dispatched.reshape(layer_tally, blocks_x, 8, blocks_y, 8)...  4.95 us
  transfers between devices with their start and end apart: 7, of which 1 were waited for; matrix products, arithmetic and copies ran while one was open for 51% of the time, Pallas kernels for 0%

commit v1 on v0

v1 whole, which is shorter than its diff:
```python
import functools

import jax
import jax.numpy as jnp
from jax import lax
from jax.experimental import pallas as pl
from jax.experimental.pallas import tpu as pltpu
from jax.sharding import PartitionSpec as P

MESH = pl.DeviceIdType.MESH
F32 = jnp.float32
BF16 = jnp.bfloat16

NU_COEF = 0.2
STEP_DT = 0.05
ATTEN_WATER = 0.06
ATTEN_CHL = 0.05
WARMING_SCALE = 0.5
GROWTH_TEMP = 0.063

LEVELS = 32
BLOCKS = 64
ROWS = 144
NT = (((1,), (1,)), ((), ()))
TN = (((0,), (0,)), ((), ()))


def iota(shape, dim):
    return lax.broadcasted_iota(jnp.int32, shape, dim)


def one_hot(mask):
    return jnp.where(mask, 1.0, 0.0).astype(BF16)


def swap_chunks(parts):
    lane = iota(parts[0].shape, 1)
    low = lane < 64
    even = (lane & 32) == 0
    a, b, c, d = parts
    a, c = jnp.where(low, a, pltpu.roll(c, 64, 1)), jnp.where(low, pltpu.roll(a, 64, 1), c)
    b, d = jnp.where(low, b, pltpu.roll(d, 64, 1)), jnp.where(low, pltpu.roll(b, 64, 1), d)
    a, b = jnp.where(even, a, pltpu.roll(b, 32, 1)), jnp.where(even, pltpu.roll(a, 96, 1), b)
    c, d = jnp.where(even, c, pltpu.roll(d, 32, 1)), jnp.where(even, pltpu.roll(c, 96, 1), d)
    return [a, b, c, d]


def exchange_kernel(
    gx_n,
    gy_n,
    t_ref,
    amb_ref,
    light_ref,
    flag_ref,
    tally_ref,
    hold_ref,
    rate_ref,
    c_hbm,
    pre_ref,
    cnt_ref,
    shift_ref,
    therm_ref,
    c_ref,
    sel_ref,
    ut_ref,
    step_ref,
    pay_ref,
    recv_ref,
    hs_ref,
    hr_ref,
    tmp_ref,
    heat_ref,
    kap_ref,
    gv_ref,
    mix_ref,
    gsum_ref,
    warm_ref,
    hxs_ref,
    hxr_ref,
    hys_ref,
    hyr_ref,
    ar_ref,
    ara_ref,
    arb_ref,
    c_sem,
    halo_s,
    halo_r,
    fs_sem,
    fr_sem,
    own_sem,
    bs_sem,
    br_sem,
    as_sem,
    ar_sem,
    gs_sem,
    gr_sem,
):
    nz = gy_n // 4
    mx = lax.axis_index("gx")
    my = lax.axis_index("gy")
    mz = my // 4
    mq = my % 4

    def c_copy(z):
        return pltpu.make_async_copy(
            c_hbm.at[pl.ds(z * 32, 32)], c_ref.at[pl.ds(z * 32, 32)], c_sem.at[z]
        )

    for q in range(nz):
        c_copy((mz - q + nz) % nz).start()

    bar = pltpu.get_barrier_semaphore()
    for d in range(1, gx_n):
        pl.semaphore_signal(
            bar, 1, device_id={"gx": (mx + d) % gx_n}, device_id_type=MESH
        )
    for d in range(1, gy_n):
        pl.semaphore_signal(
            bar, 1, device_id={"gy": (my + d) % gy_n}, device_id_type=MESH
        )

    dep = (flag_ref[...] * tally_ref[...]).astype(F32)
    hold = hold_ref[...].astype(F32)
    bi = iota((BLOCKS, BLOCKS), 0)
    bj = iota((BLOCKS, BLOCKS), 1)
    hold_b = jnp.broadcast_to(hold, (BLOCKS, BLOCKS))
    hold_c = jnp.sum(jnp.where(bi == bj, hold_b, 0.0), axis=1, keepdims=True)
    same = jnp.where((hold_c == hold_b) & (bi < bj), 1.0, 0.0)
    rank = jnp.sum(same, axis=0, keepdims=True)
    slot = hold * 8.0 + rank
    r8 = iota((8, BLOCKS), 0)
    pair = jnp.where(
        r8 == 0,
        jnp.broadcast_to(slot, (8, BLOCKS)),
        jnp.where(r8 == 1, jnp.broadcast_to(dep, (8, BLOCKS)), 0.0),
    ).astype(BF16)
    spread = one_hot(iota((BLOCKS, 512), 0) == (iota((BLOCKS, 512), 1) >> 3))
    lanes = jnp.dot(pair, spread, preferred_element_type=F32)
    slot_l = lanes[0:1]
    dep_l = lanes[1:2]
    lane8 = iota((8, 128), 1)
    dep_b = [
        jnp.broadcast_to(dep_l[:, 128 * bx : 128 * bx + 128], (8, 128)) for bx in range(4)
    ]
    cells = jnp.sum(dep, axis=1, keepdims=True) * 64.0

    hxs_ref[0, 0:32, :] = t_ref[:, 0, :]
    hxs_ref[1, 0:32, :] = t_ref[:, 31, :]
    hxs_ref[0, 32:40, :] = dep_b[0]
    hxs_ref[1, 32:40, :] = dep_b[3]

    def pack_edges(k, acc):
        low, high = acc
        low = pltpu.roll(low, 127, 1)
        high = pltpu.roll(high, 127, 1)
        for bx in range(4):
            part = t_ref[k, 8 * bx : 8 * bx + 8, :]
            place = 32 * bx + 31
            low = jnp.where(lane8 == place, pltpu.roll(part, place, 1), low)
            high = jnp.where(lane8 == place, pltpu.roll(part, (place + 1) % 128, 1), high)
        return low, high

    zero8 = jnp.zeros((8, 128), F32)
    low, high = lax.fori_loop(0, LEVELS, pack_edges, (zero8, zero8))
    dlow, dhigh = zero8, zero8
    for bx in range(4):
        dlow = jnp.where(lane8 == 32 * bx, pltpu.roll(dep_b[bx], 32 * bx, 1), dlow)
        dhigh = jnp.where(lane8 == 32 * bx, pltpu.roll(dep_b[bx], 32 * bx + 1, 1), dhigh)
    hys_ref[0, 0:8, :] = low
    hys_ref[1, 0:8, :] = high
    hys_ref[0, 8:16, :] = dlow
    hys_ref[1, 8:16, :] = dhigh

    pl.semaphore_wait(bar, gx_n - 1 + gy_n - 1)

    def halo(side):
        step = gx_n - 1 if side == 0 else 1
        stepy = gy_n - 1 if side == 0 else 1
        return (
            pltpu.make_async_remote_copy(
                hxs_ref.at[side],
                hxr_ref.at[1 - side],
                halo_s.at[side],
                halo_r.at[side],
                device_id={"gx": (mx + step) % gx_n},
                device_id_type=MESH,
            ),
            pltpu.make_async_remote_copy(
                hys_ref.at[side],
                hyr_ref.at[1 - side],
                halo_s.at[2 + side],
                halo_r.at[2 + side],
                device_id={"gy": (my + stepy) % gy_n},
                device_id_type=MESH,
            ),
        )

    halos = halo(0) + halo(1)
    for copy in halos:
        copy.start()

    lane_n = iota((1, 512), 1)
    key_l = slot_l * 8.0 + (lane_n & 7).astype(F32)

    def build_sel(z, carry):
        m = iota((256, 1), 0) + z * 256
        key = ((m >> 6) << 6) | ((m & 7) << 3) | ((m >> 3) & 7)
        sel_ref[pl.ds(pl.multiple_of(z * 256, 256), 256), :] = one_hot(
            jnp.broadcast_to(key.astype(F32), (256, 512))
            == jnp.broadcast_to(key_l, (256, 512))
        )
        return carry

    lax.fori_loop(0, nz, build_sel, 0)

    def by_lanes(field):
        return jnp.concatenate([field[8 * bx : 8 * bx + 8] for bx in range(4)], axis=1)

    aux = jnp.concatenate(
        [
            by_lanes(light_ref[...].astype(F32)),
            by_lanes(amb_ref[...].astype(F32)),
            jnp.broadcast_to(dep_l, (8, 512)),
            jnp.zeros((8, 512), F32),
        ],
        axis=0,
    ).astype(BF16)
    er = iota((256, 32), 0)
    ef = iota((256, 32), 1)
    place = one_hot(ef == jnp.where(er < 128, er >> 3, 16))
    wide = jnp.dot(place, aux, preferred_element_type=F32)
    wide = jnp.where(
        (iota((256, 512), 0) & 7) == (iota((256, 512), 1) & 7), wide, 0.0
    ).astype(BF16)
    slots = 8 * gy_n
    sel_b = one_hot(
        iota((slots, 512), 0).astype(F32) == jnp.broadcast_to(slot_l, (slots, 512))
    )
    packed_aux = lax.dot_general(sel_b, wide, NT, preferred_element_type=F32)
    packed_aux = packed_aux.reshape(gy_n, 8, 256)
    pay_ref[:, 128:144, :] = jnp.concatenate(
        [packed_aux[:, :, :128], packed_aux[:, :, 128:]], axis=1
    ).astype(BF16)

    for copy in halos:
        copy.wait_recv()

    row = iota((32, 128), 0)
    lane = iota((32, 128), 1)
    on_low_x = jnp.where(mx > 0, 1.0, 0.0)
    on_high_x = jnp.where(mx < gx_n - 1, 1.0, 0.0)
    on_low_y = jnp.where(my > 0, 1.0, 0.0)
    on_high_y = jnp.where(my < gy_n - 1, 1.0, 0.0)

    def around(field, below_row, above_row, low_h, high_h):
        up = jnp.where(row == 0, below_row, pltpu.roll(field, 1, 0))
        down = jnp.where(row == 31, above_row, pltpu.roll(field, 31, 0))
        low_v = jnp.concatenate(
            [low_h] + [pltpu.roll(low_h, 128 - 32 * bx, 1) for bx in (1, 2, 3)], axis=0
        )
        high_v = jnp.concatenate(
            [pltpu.roll(high_h, 127 - 32 * bx, 1) for bx in range(4)], axis=0
        )
        west = jnp.where(lane == 0, low_v, pltpu.roll(field, 1, 1))
        east = jnp.where(lane == 127, high_v, pltpu.roll(field, 127, 1))
        return up, down, west, east

    dep2 = jnp.concatenate(dep_b, axis=0)
    dep_n = around(
        dep2,
        hxr_ref[0, 32:33, :] * on_low_x,
        hxr_ref[1, 32:33, :] * on_high_x,
        hyr_ref[0, 8:16, :] * on_low_y,
        hyr_ref[1, 8:16, :] * on_high_y,
    )

    def stencil(kk, carry):
        low_h, high_h = carry
        done = []
        for half in range(2):
            k = kk * 2 + half
            field = t_ref[k]
            near = around(
                field,
                hxr_ref[0, pl.ds(k, 1), :],
                hxr_ref[1, pl.ds(k, 1), :],
                low_h,
                high_h,
            )
            low_h = pltpu.roll(low_h, 127, 1)
            high_h = pltpu.roll(high_h, 127, 1)
            kf = k.astype(F32)
            total = jnp.where(dep_n[0] > kf, near[0] - field, 0.0)
            for d, n in zip(dep_n[1:], near[1:]):
                total = total + jnp.where(d > kf, n - field, 0.0)
            stepped = field + NU_COEF * jnp.where(dep2 > kf, total, 0.0)
            step_ref[k] = stepped
            done.append(stepped)
        rows = pl.ds(pl.multiple_of(kk * 16, 16), 16)
        for bx in range(4):
            ut_ref[rows, 128 * bx : 128 * bx + 128] = jnp.concatenate(
                [d[8 * bx : 8 * bx + 8] for d in done], axis=0
            ).astype(BF16)
        return low_h, high_h

    lax.fori_loop(0, LEVELS // 2, stencil, (hyr_ref[0, 0:8, :], hyr_ref[1, 0:8, :]))

    def forward(other):
        return pltpu.make_async_remote_copy(
            pay_ref.at[other],
            recv_ref.at[my],
            fs_sem.at[other],
            fr_sem.at[my],
            device_id={"gy": other},
            device_id_type=MESH,
        )

    def arrival(other):
        return pltpu.make_async_remote_copy(
            pay_ref.at[other],
            recv_ref.at[other],
            fs_sem.at[other],
            fr_sem.at[other],
            device_id={"gy": other},
            device_id_type=MESH,
        )

    own = pltpu.make_async_copy(pay_ref.at[my], recv_ref.at[my], own_sem.at[0])
    for q in range(nz):
        z = (mz + q) % nz
        part = lax.dot_general(
            sel_ref[pl.ds(pl.multiple_of(z * 256, 256), 256), :],
            ut_ref[...],
            NT,
            preferred_element_type=F32,
        ).astype(BF16)
        part = part.reshape(4, 64, 256)
        pay_ref[pl.ds(z * 4, 4), 0:64, :] = part[:, :, :128]
        pay_ref[pl.ds(z * 4, 4), 64:128, :] = part[:, :, 128:]
        for d in range(4):
            if q == 0 and d == 0:
                own.start()
            else:
                forward(z * 4 + (mq + d) % 4).start()

    pi = iota((256, 256), 0)
    po = iota((256, 256), 1)
    to_columns = one_hot(po == (((pi & 31) << 3) | (pi >> 5)))
    from_columns = one_hot(pi == (((po & 31) << 3) | (po >> 5)))
    rates = jnp.concatenate([rate_ref[...]] * 32, axis=0)
    spread_r = (iota((8, 256), 1) & 7) == iota((8, 256), 0)
    rates_hi = rates.astype(BF16)
    rates_lo = (rates - rates_hi.astype(F32)).astype(BF16)
    spread_r = one_hot(spread_r)
    diagonal = (pi >> 3) == (po >> 3)
    mat_hi = jnp.where(
        diagonal, jnp.dot(rates_hi, spread_r, preferred_element_type=F32), 0.0
    ).astype(BF16)
    mat_lo = jnp.where(
        diagonal, jnp.dot(rates_lo, spread_r, preferred_element_type=F32), 0.0
    ).astype(BF16)
    upper = lane >= 64
    upper8 = lane8 >= 64
    gsum_ref[...] = jnp.zeros((8, 128), F32)

    def back(other):
        return pltpu.make_async_remote_copy(
            hs_ref.at[other],
            hr_ref.at[my],
            bs_sem.at[other],
            br_sem.at[my],
            device_id={"gy": other},
            device_id_type=MESH,
        )

    def back_arrival(other):
        return pltpu.make_async_remote_copy(
            hs_ref.at[other],
            hr_ref.at[other],
            bs_sem.at[other],
            br_sem.at[other],
            device_id={"gy": other},
            device_id_type=MESH,
        )

    own_back = pltpu.make_async_copy(hs_ref.at[my], hr_ref.at[my], own_sem.at[1])

    for q in range(nz):
        z = (mz - q + nz) % nz
        s0 = z * 32
        for d in range(4):
            if q == 0 and d == 0:
                own.wait()
            else:
                arrival(z * 4 + (mq - d + 4) % 4).wait_recv()
        c_copy(z).wait()
        blk = recv_ref[pl.ds(z * 4, 4), :, :].astype(F32)
        rows = []
        for h in range(2):
            quads = []
            for yh in range(2):
                quads.append(
                    swap_chunks(
                        [
                            blk[:, h * 64 + y * 8 : h * 64 + y * 8 + 8, :].reshape(32, 128)
                            for y in range(yh * 4, yh * 4 + 4)
                        ]
                    )
                )
            for g in range(4):
                rows.append(jnp.concatenate([quads[0][g], quads[1][g]], axis=1))
        cols = jnp.dot(
            jnp.concatenate(rows, axis=0).astype(BF16),
            to_columns,
            preferred_element_type=F32,
        )
        for g in range(8):
            tmp_ref[:, g * 256 : g * 256 + 256] = cols[g * 32 : g * 32 + 32]

        la = blk[:, 128:136, :].reshape(32, 128)
        cnt = blk[:, 136:144, :].reshape(32, 128)
        cnt_ref[pl.ds(s0, 32), :] = cnt
        la_r = pltpu.roll(la, 64, 1)
        light = jnp.where(upper, la_r, la)
        amb = jnp.where(upper, la, la_r)
        level = jnp.where(upper, 1.0, 0.0)
        run = jnp.zeros((32, 128), F32)
        prev = light
        t_next = tmp_ref[:, 0:128]
        tr_next = pltpu.roll(t_next, 64, 1)
        for i in range(16):
            at = slice(128 * i, 128 * i + 128)
            t_i, tr_i = t_next, tr_next
            if i < 15:
                t_next = tmp_ref[:, 128 * i + 128 : 128 * i + 256]
                tr_next = pltpu.roll(t_next, 64, 1)
                t_below = jnp.where(upper, tr_next, tr_i)
            else:
                t_below = jnp.where(upper, t_i, tr_i)
            atten = ATTEN_WATER + ATTEN_CHL * c_ref[pl.ds(s0, 32), 0, at]
            atten_r = pltpu.roll(atten, 64, 1)
            both = atten + atten_r
            cum = run + jnp.where(upper, both, atten)
            run = run + both
            bottom = light * jnp.exp(-cum)
            bottom_r = pltpu.roll(bottom, 64, 1)
            top = jnp.where(upper, bottom_r, prev)
            prev = bottom_r
            wet = cnt - 2.0 * i > level
            heat_ref[:, at] = jnp.where(wet, top - bottom, 0.0)
            growth = jnp.exp(GROWTH_TEMP * t_i) * top / (top + 1.0)
            gv_ref[i] = jnp.where(wet, STEP_DT * growth, 0.0)
            kap = amb * (1.0 + 0.5 * jnp.tanh(t_i - t_below))
            kap_ref[i] = jnp.where(cnt - (2.0 * i + 1.0) > level, STEP_DT * kap, 0.0)

        heat = jnp.concatenate(
            [heat_ref[:, g * 256 : g * 256 + 256] for g in range(8)], axis=0
        ).astype(BF16)
        back_cols = jnp.dot(heat, from_columns, preferred_element_type=F32)
        for h in range(2):
            quads = [
                swap_chunks(
                    [
                        back_cols[
                            (h * 4 + g) * 32 : (h * 4 + g) * 32 + 32, yh * 128 : yh * 128 + 128
                        ]
                        for g in range(4)
                    ]
                )
                for yh in range(2)
            ]
            flat = [p.reshape(4, 8, 128) for p in quads[0] + quads[1]]
            for y in range(0, 8, 2):
                hs_ref[pl.ds(z * 4, 4), h * 64 + y * 8 : h * 64 + y * 8 + 16, :] = (
                    jnp.concatenate([flat[y], flat[y + 1]], axis=1).astype(BF16)
                )
        for d in range(4):
            if q == 0 and d == 0:
                own_back.start()
            else:
                back(z * 4 + (mq - d + 4) % 4).start()

        for g in range(8):
            at = slice(256 * g, 256 * g + 256)
            c_b = c_ref[pl.ds(s0, 32), :, at].reshape(256, 256).astype(BF16)
            mix_ref[:, at] = jnp.dot(mat_hi, c_b, preferred_element_type=F32) + jnp.dot(
                mat_lo, c_b, preferred_element_type=F32
            )

        def tracers(s, acc):
            c_next = c_ref[s0 + s, :, 0:128]
            cr_next = pltpu.roll(c_next, 64, 1)
            fr_prev = jnp.zeros((8, 128), F32)
            for i in range(16):
                at = slice(128 * i, 128 * i + 128)
                c_i, cr_i = c_next, cr_next
                if i < 15:
                    c_next = c_ref[s0 + s, :, 128 * i + 128 : 128 * i + 256]
                    cr_next = pltpu.roll(c_next, 64, 1)
                below = jnp.where(upper8, cr_next, cr_i)
                flux = kap_ref[i, pl.ds(s, 1), :] * (below - c_i)
                flux_r = pltpu.roll(flux, 64, 1)
                above = jnp.where(upper8, flux_r, fr_prev)
                fr_prev = flux_r
                grown = (
                    gv_ref[i, pl.ds(s, 1), :]
                    * mix_ref[pl.ds(pl.multiple_of(s * 8, 8), 8), at]
                )
                acc = acc + grown
                pre_ref[s0 + s, :, at] = c_i + ((flux - above) + grown)
            return acc

        gsum_ref[...] = lax.fori_loop(0, 32, tracers, gsum_ref[...])

    ar_ref[0, 0:8, :] = gsum_ref[...]
    ar_ref[0, 8:16, :] = jnp.broadcast_to(cells, (8, 128))

    def gx_send(other):
        return pltpu.make_async_remote_copy(
            ar_ref.at[0],
            ara_ref.at[mx],
            as_sem.at[other],
            ar_sem.at[mx],
            device_id={"gx": other},
            device_id_type=MESH,
        )

    def gx_arrival(other):
        return pltpu.make_async_remote_copy(
            ar_ref.at[0],
            ara_ref.at[other],
            as_sem.at[other],
            ar_sem.at[other],
            device_id={"gx": other},
            device_id_type=MESH,
        )

    def gy_send(other):
        return pltpu.make_async_remote_copy(
            ar_ref.at[1],
            arb_ref.at[my],
            gs_sem.at[other],
            gr_sem.at[my],
            device_id={"gy": other},
            device_id_type=MESH,
        )

    def gy_arrival(other):
        return pltpu.make_async_remote_copy(
            ar_ref.at[1],
            arb_ref.at[other],
            gs_sem.at[other],
            gr_sem.at[other],
            device_id={"gy": other},
            device_id_type=MESH,
        )

    for d in range(1, gx_n):
        gx_send((mx + d) % gx_n).start()
    ara_ref[mx] = ar_ref[0]
    for d in range(1, gx_n):
        gx_arrival((mx + d) % gx_n).wait_recv()
    ar_ref[1] = jnp.sum(ara_ref[...], axis=0)
    for d in range(1, gy_n):
        gy_send((my + d) % gy_n).start()
    arb_ref[my] = ar_ref[1]

    for q in range(nz):
        z = (mz + q) % nz
        for d in range(4):
            if q == 0 and d == 0:
                own_back.wait()
            else:
                back_arrival(z * 4 + (mq + d) % 4).wait_recv()
        got = hr_ref[pl.ds(z * 4, 4), :, :]
        sel = sel_ref[pl.ds(pl.multiple_of(z * 256, 256), 256), :]
        for h in range(2):
            lhs = got[:, h * 64 : h * 64 + 64, :].reshape(256, 128)
            warm = lax.dot_general(lhs, sel, TN, preferred_element_type=F32)
            rows_h = slice(128 * h, 128 * h + 128)
            if q == 0:
                warm_ref[rows_h, :] = warm
            else:
                warm_ref[rows_h, :] = warm_ref[rows_h, :] + warm

    def finish(k, carry):
        part = warm_ref[pl.ds(pl.multiple_of(k * 8, 8), 8), :]
        for bx in range(4):
            therm_ref[k, 8 * bx : 8 * bx + 8, :] = (
                step_ref[k, 8 * bx : 8 * bx + 8, :]
                + WARMING_SCALE * part[:, 128 * bx : 128 * bx + 128]
            )
        return carry

    lax.fori_loop(0, LEVELS, finish, 0)

    for d in range(1, gy_n):
        gy_arrival((my + d) % gy_n).wait_recv()
    total = jnp.sum(arb_ref[...], axis=0)
    grown = jnp.sum(total[0:8], axis=1, keepdims=True)
    shift_ref[...] = -(jnp.broadcast_to(grown, (8, 128)) / jnp.maximum(total[8:16], 1.0))

    for copy in halos:
        copy.wait_send()
    for d in range(1, gy_n):
        forward((my + d) % gy_n).wait_send()
        back((my + d) % gy_n).wait_send()
        gy_send((my + d) % gy_n).wait_send()
    for d in range(1, gx_n):
        gx_send((mx + d) % gx_n).wait_send()


def finish_kernel(pre_ref, cnt_ref, shift_ref, therm_ref, out_ref, thout_ref, buf_ref, sem):
    upper = iota((8, 128), 1) >= 64
    level = jnp.where(upper, 1.0, 0.0)
    n = pre_ref.shape[0] // 16
    thermal = pltpu.make_async_copy(therm_ref, thout_ref, sem.at[2])
    thermal.start()
    shift = shift_ref[...]

    def out_copy(c):
        return pltpu.make_async_copy(
            buf_ref.at[c % 2], out_ref.at[pl.ds(c * 16, 16)], sem.at[c % 2]
        )

    for c in range(n):
        if c >= 2:
            out_copy(c - 2).wait()

        def one(s, carry):
            cnt = cnt_ref[pl.ds(c * 16 + s, 1), :]
            for i in range(16):
                at = slice(128 * i, 128 * i + 128)
                buf_ref[c % 2, s, :, at] = pre_ref[c * 16 + s, :, at] + jnp.where(
                    cnt - 2.0 * i > level, shift, 0.0
                )
            return carry

        lax.fori_loop(0, 16, one, 0)
        out_copy(c).start()
    for c in range(max(n - 2, 0), n):
        out_copy(c).wait()
    thermal.wait()


def solution(mesh):
    gx_n = mesh.shape["gx"]
    gy_n = mesh.shape["gy"]
    slots = 8 * gy_n

    def on_device(thermal, amb, light, flags, tally, hold, solutes, rates):
        dma = pltpu.SemaphoreType.DMA
        vmem = pl.BlockSpec(memory_space=pltpu.VMEM)
        hbm = pl.BlockSpec(memory_space=pl.ANY)
        tracers = solutes.reshape(slots, 8, 2048)
        pre, cnt, shift, therm = pl.pallas_call(
            functools.partial(exchange_kernel, gx_n, gy_n),
            out_shape=[
                pltpu.VMEM((slots, 8, 2048), F32),
                pltpu.VMEM((slots, 128), F32),
                pltpu.VMEM((8, 128), F32),
                pltpu.VMEM((32, 32, 128), F32),
            ],
            in_specs=[vmem] * 7 + [hbm],
            out_specs=[vmem] * 4,
            scratch_shapes=[
                pltpu.VMEM((slots, 8, 2048), F32),
                pltpu.VMEM((64 * gy_n, 512), BF16),
                pltpu.VMEM((256, 512), BF16),
                pltpu.VMEM((32, 32, 128), F32),
                pltpu.VMEM((gy_n, ROWS, 128), BF16),
                pltpu.VMEM((gy_n, ROWS, 128), BF16),
                pltpu.VMEM((gy_n, 128, 128), BF16),
                pltpu.VMEM((gy_n, 128, 128), BF16),
                pltpu.VMEM((32, 2048), F32),
                pltpu.VMEM((32, 2048), F32),
                pltpu.VMEM((16, 32, 128), F32),
                pltpu.VMEM((16, 32, 128), F32),
                pltpu.VMEM((256, 2048), F32),
                pltpu.VMEM((8, 128), F32),
                pltpu.VMEM((256, 512), F32),
                pltpu.VMEM((2, 40, 128), F32),
                pltpu.VMEM((2, 40, 128), F32),
                pltpu.VMEM((2, 16, 128), F32),
                pltpu.VMEM((2, 16, 128), F32),
                pltpu.VMEM((2, 16, 128), F32),
                pltpu.VMEM((gx_n, 16, 128), F32),
                pltpu.VMEM((gy_n, 16, 128), F32),
                dma((gy_n // 4,)),
                dma((4,)),
                dma((4,)),
                dma((gy_n,)),
                dma((gy_n,)),
                dma((2,)),
                dma((gy_n,)),
                dma((gy_n,)),
                dma((gx_n,)),
                dma((gx_n,)),
                dma((gy_n,)),
                dma((gy_n,)),
            ],
            compiler_params=pltpu.CompilerParams(
                collective_id=0, has_side_effects=True, vmem_limit_bytes=40 * 1024 * 1024
            ),
            name="exchange",
        )(
            thermal,
            amb,
            light,
            flags.reshape(1, BLOCKS),
            tally.reshape(1, BLOCKS),
            hold.reshape(1, BLOCKS),
            rates,
            tracers,
        )
        out, therm_out = pl.pallas_call(
            finish_kernel,
            out_shape=[
                jax.ShapeDtypeStruct((slots, 8, 2048), F32),
                jax.ShapeDtypeStruct((32, 32, 128), F32),
            ],
            in_specs=[vmem] * 4,
            out_specs=[hbm] * 2,
            scratch_shapes=[pltpu.VMEM((2, 16, 8, 2048), F32), dma((3,))],
            compiler_params=pltpu.CompilerParams(vmem_limit_bytes=16 * 1024 * 1024),
            name="finish",
        )(pre, cnt, shift, therm)
        return therm_out, out.reshape(solutes.shape)

    return jax.shard_map(
        on_device,
        mesh=mesh,
        in_specs=(
            P(None, "gx", "gy"),
            P("gx", "gy"),
            P("gx", "gy"),
            P("gx", "gy", None),
            P("gx", "gy", None),
            P("gx", "gy", None, None),
            P("gx", "gy", None, None, None),
            P(),
        ),
        out_specs=(P(None, "gx", "gy"), P("gx", "gy", None, None, None)),
        check_vma=False,
    )
```

time: 179 us -> 68.3 us (0.38)
  the two profiles are of different devices: /device:TPU:0 before, /device:TPU:1 now
where the time goes in v1:
time: 68.3 us; the launch traced here: 68 us
  Pallas kernels  62.3 us (91%)
  local copies, waits for them, and re-layouts  5.08 us (7%)
    pallas_call x1, Pallas kernels, on_device(): pl.pallas_call(functools.partial(exchange_kernel, gx_n, gy_n), out_shape=...  57.1 us
    pallas_call x1, Pallas kernels, on_device(): pl.pallas_call(finish_kernel, out_shape=[jax.ShapeDtypeStruct((slots, 8,...  5.19 us
    unnamed x14, local copies, waits for them, and re-layouts  5.08 us

profile of v1, /device:TPU:1, one launch (start us, length us, event | category | flops | bytes accessed | tf_op | source)
XLA Modules:
  0.0 68.0 jit_solution(17568368475074277724)
XLA Ops:
  0.6 0.0 copy-start
  0.6 1.0 %copy-done = f32[32,32,128]{2,1,0:T(8,128)S(1)} copy-done((f32[32,32,128]{2,1,0:T(8,128)S(1)}, f32[32,32,128]{2,1,0:T(8,128)}, u32[]{:S(2)}) %copy-start) | copy-done | bytes 524312
  1.7 0.0 copy-start.1
  1.7 0.7 %copy-done.1 = bf16[32,128]{1,0:T(8,128)(2,1)S(1)} copy-done((bf16[32,128]{1,0:T(8,128)(2,1)S(1)}, bf16[32,128]{1,0:T(8,128)(2,1)}, u32[]{:S(2)}) %copy-start.1) | copy-done | bytes 8216
  2.4 0.0 copy-start.2
  2.4 0.7 %copy-done.2 = bf16[32,128]{1,0:T(8,128)(2,1)S(1)} copy-done((bf16[32,128]{1,0:T(8,128)(2,1)S(1)}, bf16[32,128]{1,0:T(8,128)(2,1)}, u32[]{:S(2)}) %copy-start.2) | copy-done | bytes 8216
  3.1 0.0 copy-start.3
  3.1 0.7 %copy-done.3 = f32[8,8]{1,0:T(8,128)S(1)} copy-done((f32[8,8]{1,0:T(8,128)S(1)}, f32[8,8]{1,0:T(8,128)}, u32[]{:S(2)}) %copy-start.3) | copy-done | bytes 280
  3.8 0.0 copy-start.4
  3.8 0.7 copy-done.4
  4.4 0.0 copy-start.5
  4.4 0.7 copy-done.5
  5.1 0.0 copy-start.6
  5.1 0.7 copy-done.6
  5.7 57.1 %exchange.1 = (f32[128,8,2048]{2,1,0:T(8,128)S(1)}, f32[128,128]{1,0:T(8,128)S(1)}, f32[8,128]{1,0:T(8,128)S(1)}, f32[32,32,128]{2,1,0:T(8,128)S(1)}) custom-call(f32[32,32,128]{2,1,0:T(8,128)S(1)} %copy-done, bf16[32,128]{1,0:T(8,128)(2,1)S(1)} %copy-done.1, bf16[32,128]{1,0:T(8,128)(2,1)S(1)} %copy-done.2, s32[1,64]{1,0:T(1,128)S(1)} %bitcast.5, ...), custom_call_target="tpu_custom_call" | custom-call | tf_op jit(solution)/shard_map/exchange/pallas_call | solution.py:656
  62.8 5.2 %finish.1 = (f32[128,8,2048]{2,1,0:T(8,128)}, f32[32,32,128]{2,1,0:T(8,128)}) custom-call(f32[128,8,2048]{2,1,0:T(8,128)S(1)} %get-tuple-element.8.pre_ref, f32[128,128]{1,0:T(8,128)S(1)} %get-tuple-element.9.cnt_ref, f32[8,128]{1,0:T(8,128)S(1)} %get-tuple-element.10.shift_ref, f32[32,32,128]{2,1,0:T(8,128)S(1)} %get-tuple-element.11.therm_ref), custom_call_target="tpu_custom_call" | custom-call | tf_op jit(solution)/shard_map/finish/pallas_call | solution.py:716
Async XLA Ops:
  0.6 1.0 %copy-start = (f32[32,32,128]{2,1,0:T(8,128)S(1)}, f32[32,32,128]{2,1,0:T(8,128)}, u32[]{:S(2)}) copy-start(f32[32,32,128]{2,1,0:T(8,128)} %t_ref.1) | copy-start | bytes 1572868
  1.7 0.7 %copy-start.1 = (bf16[32,128]{1,0:T(8,128)(2,1)S(1)}, bf16[32,128]{1,0:T(8,128)(2,1)}, u32[]{:S(2)}) copy-start(bf16[32,128]{1,0:T(8,128)(2,1)} %amb_ref.1) | copy-start | bytes 24580
  2.4 0.7 %copy-start.2 = (bf16[32,128]{1,0:T(8,128)(2,1)S(1)}, bf16[32,128]{1,0:T(8,128)(2,1)}, u32[]{:S(2)}) copy-start(bf16[32,128]{1,0:T(8,128)(2,1)} %light_ref.1) | copy-start | bytes 24580
  3.1 0.7 %copy-start.3 = (f32[8,8]{1,0:T(8,128)S(1)}, f32[8,8]{1,0:T(8,128)}, u32[]{:S(2)}) copy-start(f32[8,8]{1,0:T(8,128)} %rate_ref.1) | copy-start | bytes 772
  3.8 0.7 copy-start.4
  4.4 0.7 copy-start.5
  5.1 0.7 copy-start.6

commit v2 on v1

--- a/solution.py
+++ b/solution.py
@@ -21,6 +21,11 @@
 LEVELS = 32
 BLOCKS = 64
 ROWS = 144
+UNROLL = 4
+LEVEL_STEP = 8
+OUT_STEP = 8
+OUT_CHUNK = 16
+OUT_BUFS = 8
 NT = (((1,), (1,)), ((), ()))
 TN = (((0,), (0,)), ((), ()))
 
@@ -48,6 +53,18 @@
 def exchange_kernel(
     gx_n,
     gy_n,
+    t_hbm,
+    amb_hbm,
+    light_hbm,
+    flag_hbm,
+    tally_hbm,
+    hold_hbm,
+    rate_hbm,
+    c_hbm,
+    pre_ref,
+    cnt_ref,
+    shift_ref,
+    therm_ref,
     t_ref,
     amb_ref,
     light_ref,
@@ -55,11 +72,6 @@
     tally_ref,
     hold_ref,
     rate_ref,
-    c_hbm,
-    pre_ref,
-    cnt_ref,
-    shift_ref,
-    therm_ref,
     c_ref,
     sel_ref,
     ut_ref,
@@ -71,9 +83,9 @@
     tmp_ref,
     heat_ref,
     kap_ref,
+    kup_ref,
     gv_ref,
     mix_ref,
-    gsum_ref,
     warm_ref,
     hxs_ref,
     hxr_ref,
@@ -82,6 +94,7 @@
     ar_ref,
     ara_ref,
     arb_ref,
+    in_sem,
     c_sem,
     halo_s,
     halo_r,
@@ -106,8 +119,22 @@
             c_hbm.at[pl.ds(z * 32, 32)], c_ref.at[pl.ds(z * 32, 32)], c_sem.at[z]
         )
 
-    for q in range(nz):
-        c_copy((mz - q + nz) % nz).start()
+    loads = [
+        pltpu.make_async_copy(src, dst, in_sem.at[n])
+        for n, (src, dst) in enumerate(
+            (
+                (t_hbm, t_ref),
+                (flag_hbm, flag_ref),
+                (tally_hbm, tally_ref),
+                (hold_hbm, hold_ref),
+                (amb_hbm, amb_ref),
+                (light_hbm, light_ref),
+                (rate_hbm, rate_ref),
+            )
+        )
+    ]
+    for copy in loads:
+        copy.start()
 
     bar = pltpu.get_barrier_semaphore()
     for d in range(1, gx_n):
@@ -118,6 +145,11 @@
         pl.semaphore_signal(
             bar, 1, device_id={"gy": (my + d) % gy_n}, device_id_type=MESH
         )
+
+    for copy in loads:
+        copy.wait()
+    for q in range(nz):
+        c_copy((mz - q + nz) % nz).start()
 
     dep = (flag_ref[...] * tally_ref[...]).astype(F32)
     hold = hold_ref[...].astype(F32)
@@ -149,19 +181,27 @@
     hxs_ref[0, 32:40, :] = dep_b[0]
     hxs_ref[1, 32:40, :] = dep_b[3]
 
-    def pack_edges(k, acc):
-        low, high = acc
-        low = pltpu.roll(low, 127, 1)
-        high = pltpu.roll(high, 127, 1)
+    zero8 = jnp.zeros((8, 128), F32)
+    low4, high4 = [zero8] * 4, [zero8] * 4
+    for k in range(LEVELS):
         for bx in range(4):
             part = t_ref[k, 8 * bx : 8 * bx + 8, :]
-            place = 32 * bx + 31
-            low = jnp.where(lane8 == place, pltpu.roll(part, place, 1), low)
-            high = jnp.where(lane8 == place, pltpu.roll(part, (place + 1) % 128, 1), high)
-        return low, high
-
-    zero8 = jnp.zeros((8, 128), F32)
-    low, high = lax.fori_loop(0, LEVELS, pack_edges, (zero8, zero8))
+            place = 32 * bx + k
+            low4[bx] = jnp.where(lane8 == place, pltpu.roll(part, place, 1), low4[bx])
+            high4[bx] = jnp.where(
+                lane8 == place, pltpu.roll(part, (place + 1) % 128, 1), high4[bx]
+            )
+    quarter = lane8 >> 5
+    low = jnp.where(
+        quarter < 2,
+        jnp.where(quarter == 0, low4[0], low4[1]),
+        jnp.where(quarter == 2, low4[2], low4[3]),
+    )
+    high = jnp.where(
+        quarter < 2,
+        jnp.where(quarter == 0, high4[0], high4[1]),
+        jnp.where(quarter == 2, high4[2], high4[3]),
+    )
     dlow, dhigh = zero8, zero8
     for bx in range(4):
         dlow = jnp.where(lane8 == 32 * bx, pltpu.roll(dep_b[bx], 32 * bx, 1), dlow)
@@ -277,8 +317,8 @@
     def stencil(kk, carry):
         low_h, high_h = carry
         done = []
-        for half in range(2):
-            k = kk * 2 + half
+        for part in range(LEVEL_STEP):
+            k = kk * LEVEL_STEP + part
             field = t_ref[k]
             near = around(
                 field,
@@ -296,14 +336,16 @@
             stepped = field + NU_COEF * jnp.where(dep2 > kf, total, 0.0)
             step_ref[k] = stepped
             done.append(stepped)
-        rows = pl.ds(pl.multiple_of(kk * 16, 16), 16)
+        size = 8 * LEVEL_STEP
+        rows = pl.ds(pl.multiple_of(kk * size, size), size)
         for bx in range(4):
             ut_ref[rows, 128 * bx : 128 * bx + 128] = jnp.concatenate(
                 [d[8 * bx : 8 * bx + 8] for d in done], axis=0
             ).astype(BF16)
         return low_h, high_h
 
-    lax.fori_loop(0, LEVELS // 2, stencil, (hyr_ref[0, 0:8, :], hyr_ref[1, 0:8, :]))
+    lax.fori_loop(
+        0, LEVELS // LEVEL_STEP, stencil, (hyr_ref[0, 0:8, :], hyr_ref[1, 0:8, :]))
 
     def forward(other):
         return pltpu.make_async_remote_copy(
@@ -361,7 +403,7 @@
     ).astype(BF16)
     upper = lane >= 64
     upper8 = lane8 >= 64
-    gsum_ref[...] = jnp.zeros((8, 128), F32)
+    sums = (zero8,) * 4
 
     def back(other):
         return pltpu.make_async_remote_copy(
@@ -384,6 +426,53 @@
         )
 
     own_back = pltpu.make_async_copy(hs_ref.at[my], hr_ref.at[my], own_sem.at[1])
+
+    def gx_send(other):
+        return pltpu.make_async_remote_copy(
+            ar_ref.at[0],
+            ara_ref.at[mx],
+            as_sem.at[other],
+            ar_sem.at[mx],
+            device_id={"gx": other},
+            device_id_type=MESH,
+        )
+
+    def gx_arrival(other):
+        return pltpu.make_async_remote_copy(
+            ar_ref.at[0],
+            ara_ref.at[other],
+            as_sem.at[other],
+            ar_sem.at[other],
+            device_id={"gx": other},
+            device_id_type=MESH,
+        )
+
+    def gy_send(other):
+        return pltpu.make_async_remote_copy(
+            ar_ref.at[1],
+            arb_ref.at[my],
+            gs_sem.at[other],
+            gr_sem.at[my],
+            device_id={"gy": other},
+            device_id_type=MESH,
+        )
+
+    def gy_arrival(other):
+        return pltpu.make_async_remote_copy(
+            ar_ref.at[1],
+            arb_ref.at[other],
+            gs_sem.at[other],
+            gr_sem.at[other],
+            device_id={"gy": other},
+            device_id_type=MESH,
+        )
+
+    def gx_sums(sums):
+        ar_ref[0, 0:8, :] = (sums[0] + sums[1]) + (sums[2] + sums[3])
+        ar_ref[0, 8:16, :] = jnp.broadcast_to(cells, (8, 128))
+        for d in range(1, gx_n):
+            gx_send((mx + d) % gx_n).start()
+        ara_ref[mx] = ar_ref[0]
 
     for q in range(nz):
         z = (mz - q + nz) % nz
@@ -426,6 +515,7 @@
         level = jnp.where(upper, 1.0, 0.0)
         run = jnp.zeros((32, 128), F32)
         prev = light
+        kap_prev = jnp.zeros((32, 128), F32)
         t_next = tmp_ref[:, 0:128]
         tr_next = pltpu.roll(t_next, 64, 1)
         for i in range(16):
@@ -449,9 +539,13 @@
             wet = cnt - 2.0 * i > level
             heat_ref[:, at] = jnp.where(wet, top - bottom, 0.0)
             growth = jnp.exp(GROWTH_TEMP * t_i) * top / (top + 1.0)
-            gv_ref[i] = jnp.where(wet, STEP_DT * growth, 0.0)
+            gv_ref[i, 0:32] = jnp.where(wet, STEP_DT * growth, 0.0)
             kap = amb * (1.0 + 0.5 * jnp.tanh(t_i - t_below))
-            kap_ref[i] = jnp.where(cnt - (2.0 * i + 1.0) > level, STEP_DT * kap, 0.0)
+            kap = jnp.where(cnt - (2.0 * i + 1.0) > level, STEP_DT * kap, 0.0)
+            kap_r = pltpu.roll(kap, 64, 1)
+            kap_ref[i, 0:32] = kap
+            kup_ref[i, 0:32] = jnp.where(upper, kap_r, kap_prev)
+            kap_prev = kap_r
 
         heat = jnp.concatenate(
             [heat_ref[:, g * 256 : g * 256 + 256] for g in range(8)], axis=0
@@ -487,77 +581,53 @@
                 mat_lo, c_b, preferred_element_type=F32
             )
 
-        def tracers(s, acc):
-            c_next = c_ref[s0 + s, :, 0:128]
-            cr_next = pltpu.roll(c_next, 64, 1)
-            fr_prev = jnp.zeros((8, 128), F32)
-            for i in range(16):
-                at = slice(128 * i, 128 * i + 128)
-                c_i, cr_i = c_next, cr_next
-                if i < 15:
-                    c_next = c_ref[s0 + s, :, 128 * i + 128 : 128 * i + 256]
-                    cr_next = pltpu.roll(c_next, 64, 1)
-                below = jnp.where(upper8, cr_next, cr_i)
-                flux = kap_ref[i, pl.ds(s, 1), :] * (below - c_i)
-                flux_r = pltpu.roll(flux, 64, 1)
-                above = jnp.where(upper8, flux_r, fr_prev)
-                fr_prev = flux_r
-                grown = (
-                    gv_ref[i, pl.ds(s, 1), :]
-                    * mix_ref[pl.ds(pl.multiple_of(s * 8, 8), 8), at]
-                )
-                acc = acc + grown
-                pre_ref[s0 + s, :, at] = c_i + ((flux - above) + grown)
-            return acc
-
-        gsum_ref[...] = lax.fori_loop(0, 32, tracers, gsum_ref[...])
-
-    ar_ref[0, 0:8, :] = gsum_ref[...]
-    ar_ref[0, 8:16, :] = jnp.broadcast_to(cells, (8, 128))
-
-    def gx_send(other):
-        return pltpu.make_async_remote_copy(
-            ar_ref.at[0],
-            ara_ref.at[mx],
-            as_sem.at[other],
-            ar_sem.at[mx],
-            device_id={"gx": other},
-            device_id_type=MESH,
-        )
-
-    def gx_arrival(other):
-        return pltpu.make_async_remote_copy(
-            ar_ref.at[0],
-            ara_ref.at[other],
-            as_sem.at[other],
-            ar_sem.at[other],
-            device_id={"gx": other},
-            device_id_type=MESH,
-        )
-
-    def gy_send(other):
-        return pltpu.make_async_remote_copy(
-            ar_ref.at[1],
-            arb_ref.at[my],
-            gs_sem.at[other],
-            gr_sem.at[my],
-            device_id={"gy": other},
-            device_id_type=MESH,
-        )
-
-    def gy_arrival(other):
-        return pltpu.make_async_remote_copy(
-            ar_ref.at[1],
-            arb_ref.at[other],
-            gs_sem.at[other],
-            gr_sem.at[other],
-            device_id={"gy": other},
-            device_id_type=MESH,
-        )
-
-    for d in range(1, gx_n):
-        gx_send((mx + d) % gx_n).start()
-    ara_ref[mx] = ar_ref[0]
+        def row_of(ref, i, s):
+            return ref[i, pl.ds(s, 8, stride=0), :]
+
+        def mix_of(i, s):
+            return mix_ref[
+                pl.ds(pl.multiple_of(s * 8, 8), 8), 128 * i : 128 * i + 128
+            ]
+
+        def grow(step, acc):
+            acc = list(acc)
+            for u in range(UNROLL):
+                s = step * UNROLL + u
+                for i in range(16):
+                    acc[i % 4] = acc[i % 4] + row_of(gv_ref, i, s) * mix_of(i, s)
+            return tuple(acc)
+
+        def tracers(counted, step, acc):
+            acc = list(acc)
+            for u in range(UNROLL):
+                s = step * UNROLL + u
+                c_next = c_ref[s0 + s, :, 0:128]
+                cr_next = pltpu.roll(c_next, 64, 1)
+                cr_i = cr_next
+                for i in range(16):
+                    at = slice(128 * i, 128 * i + 128)
+                    cr_prev = cr_i
+                    c_i, cr_i = c_next, cr_next
+                    if i < 15:
+                        c_next = c_ref[s0 + s, :, 128 * i + 128 : 128 * i + 256]
+                        cr_next = pltpu.roll(c_next, 64, 1)
+                    below = jnp.where(upper8, cr_next, cr_i)
+                    above = jnp.where(upper8, cr_i, cr_prev)
+                    grown = row_of(gv_ref, i, s) * mix_of(i, s)
+                    if counted:
+                        acc[i % 4] = acc[i % 4] + grown
+                    pre_ref[s0 + s, :, at] = (c_i + row_of(kap_ref, i, s) * (below - c_i)) + (
+                        row_of(kup_ref, i, s) * (above - c_i) + grown
+                    )
+            return tuple(acc)
+
+        last = q == nz - 1
+        steps = 32 // UNROLL
+        if last:
+            sums = lax.fori_loop(0, steps, grow, sums)
+            gx_sums(sums)
+        sums = lax.fori_loop(0, steps, functools.partial(tracers, not last), sums)
+
     for d in range(1, gx_n):
         gx_arrival((mx + d) % gx_n).wait_recv()
     ar_ref[1] = jnp.sum(ara_ref[...], axis=0)
@@ -611,34 +681,37 @@
 
 
 def finish_kernel(pre_ref, cnt_ref, shift_ref, therm_ref, out_ref, thout_ref, buf_ref, sem):
-    upper = iota((8, 128), 1) >= 64
-    level = jnp.where(upper, 1.0, 0.0)
-    n = pre_ref.shape[0] // 16
-    thermal = pltpu.make_async_copy(therm_ref, thout_ref, sem.at[2])
+    level = jnp.where(iota((8, 128), 1) >= 64, 1.0, 0.0)
+    n = pre_ref.shape[0] // OUT_CHUNK
+    thermal = pltpu.make_async_copy(therm_ref, thout_ref, sem.at[OUT_BUFS])
     thermal.start()
     shift = shift_ref[...]
 
     def out_copy(c):
         return pltpu.make_async_copy(
-            buf_ref.at[c % 2], out_ref.at[pl.ds(c * 16, 16)], sem.at[c % 2]
+            buf_ref.at[c % OUT_BUFS],
+            out_ref.at[pl.ds(c * OUT_CHUNK, OUT_CHUNK)],
+            sem.at[c % OUT_BUFS],
         )
 
     for c in range(n):
-        if c >= 2:
-            out_copy(c - 2).wait()
-
-        def one(s, carry):
-            cnt = cnt_ref[pl.ds(c * 16 + s, 1), :]
-            for i in range(16):
-                at = slice(128 * i, 128 * i + 128)
-                buf_ref[c % 2, s, :, at] = pre_ref[c * 16 + s, :, at] + jnp.where(
-                    cnt - 2.0 * i > level, shift, 0.0
-                )
+        if c >= OUT_BUFS:
+            out_copy(c - OUT_BUFS).wait()
+
+        def some(step, carry):
+            for u in range(OUT_STEP):
+                s = step * OUT_STEP + u
+                wet = cnt_ref[pl.ds(c * OUT_CHUNK + s, 8, stride=0), :] - level
+                for i in range(16):
+                    at = slice(128 * i, 128 * i + 128)
+                    buf_ref[c % OUT_BUFS, s, :, at] = pre_ref[
+                        c * OUT_CHUNK + s, :, at
+                    ] + jnp.where(wet > 2.0 * i, shift, 0.0)
             return carry
 
-        lax.fori_loop(0, 16, one, 0)
+        lax.fori_loop(0, OUT_CHUNK // OUT_STEP, some, 0)
         out_copy(c).start()
-    for c in range(max(n - 2, 0), n):
+    for c in range(max(n - OUT_BUFS, 0), n):
         out_copy(c).wait()
     thermal.wait()
 
@@ -651,19 +724,26 @@
     def on_device(thermal, amb, light, flags, tally, hold, solutes, rates):
         dma = pltpu.SemaphoreType.DMA
         vmem = pl.BlockSpec(memory_space=pltpu.VMEM)
-        hbm = pl.BlockSpec(memory_space=pl.ANY)
+        hbm = pl.BlockSpec(memory_space=pltpu.HBM)
         tracers = solutes.reshape(slots, 8, 2048)
         pre, cnt, shift, therm = pl.pallas_call(
             functools.partial(exchange_kernel, gx_n, gy_n),
             out_shape=[
                 pltpu.VMEM((slots, 8, 2048), F32),
-                pltpu.VMEM((slots, 128), F32),
+                pltpu.VMEM((slots + 8, 128), F32),
                 pltpu.VMEM((8, 128), F32),
                 pltpu.VMEM((32, 32, 128), F32),
             ],
-            in_specs=[vmem] * 7 + [hbm],
+            in_specs=[hbm] * 8,
             out_specs=[vmem] * 4,
             scratch_shapes=[
+                pltpu.VMEM((32, 32, 128), F32),
+                pltpu.VMEM((32, 128), BF16),
+                pltpu.VMEM((32, 128), BF16),
+                pltpu.VMEM((1, BLOCKS), jnp.int32),
+                pltpu.VMEM((1, BLOCKS), jnp.int32),
+                pltpu.VMEM((1, BLOCKS), jnp.int32),
+                pltpu.VMEM((8, 8), F32),
                 pltpu.VMEM((slots, 8, 2048), F32),
                 pltpu.VMEM((64 * gy_n, 512), BF16),
                 pltpu.VMEM((256, 512), BF16),
@@ -674,10 +754,10 @@
                 pltpu.VMEM((gy_n, 128, 128), BF16),
                 pltpu.VMEM((32, 2048), F32),
                 pltpu.VMEM((32, 2048), F32),
-                pltpu.VMEM((16, 32, 128), F32),
-                pltpu.VMEM((16, 32, 128), F32),
+                pltpu.VMEM((16, 40, 128), F32),
+                pltpu.VMEM((16, 40, 128), F32),
+                pltpu.VMEM((16, 40, 128), F32),
                 pltpu.VMEM((256, 2048), F32),
-                pltpu.VMEM((8, 128), F32),
                 pltpu.VMEM((256, 512), F32),
                 pltpu.VMEM((2, 40, 128), F32),
                 pltpu.VMEM((2, 40, 128), F32),
@@ -686,6 +766,7 @@
                 pltpu.VMEM((2, 16, 128), F32),
                 pltpu.VMEM((gx_n, 16, 128), F32),
                 pltpu.VMEM((gy_n, 16, 128), F32),
+                dma((7,)),
                 dma((gy_n // 4,)),
                 dma((4,)),
                 dma((4,)),
@@ -704,14 +785,19 @@
             ),
             name="exchange",
         )(
-            thermal,
-            amb,
-            light,
-            flags.reshape(1, BLOCKS),
-            tally.reshape(1, BLOCKS),
-            hold.reshape(1, BLOCKS),
-            rates,
-            tracers,
+            *(
+                pltpu.with_memory_space_constraint(a, pltpu.HBM)
+                for a in (
+                    thermal,
+                    amb,
+                    light,
+                    flags.reshape(1, BLOCKS),
+                    tally.reshape(1, BLOCKS),
+                    hold.reshape(1, BLOCKS),
+                    rates,
+                    tracers,
+                )
+            )
         )
         out, therm_out = pl.pallas_call(
             finish_kernel,
@@ -721,7 +807,10 @@
             ],
             in_specs=[vmem] * 4,
             out_specs=[hbm] * 2,
-            scratch_shapes=[pltpu.VMEM((2, 16, 8, 2048), F32), dma((3,))],
+            scratch_shapes=[
+                pltpu.VMEM((OUT_BUFS, OUT_CHUNK, 8, 2048), F32),
+                dma((OUT_BUFS + 1,)),
+            ],
             compiler_params=pltpu.CompilerParams(vmem_limit_bytes=16 * 1024 * 1024),
             name="finish",
         )(pre, cnt, shift, therm)

time: 68.3 us -> 44.2 us (0.65)
  Pallas kernels: 62.3 us -> 43.5 us
  local copies, waits for them, and re-layouts: 5.08 us -> 0 us
    pallas_call x1, Pallas kernels: 57.1 us -> 39.9 us  [on_device(): pl.pallas_call(functools.partial(exchange_kernel, gx_n, gy_n), out_shape=...]
    unnamed x14 -> x0, local copies, waits for them, and re-layouts: 5.08 us -> none
    pallas_call x1, Pallas kernels: 5.19 us -> 3.55 us  [on_device(): pl.pallas_call(finish_kernel, out_shape=[jax.ShapeDtypeStruct((slots, 8,...]
where the time goes in v2:
time: 44.2 us; the launch traced here: 44.1 us
  Pallas kernels  43.5 us (98%)
  between operations  0.64 us (1%)
    pallas_call x1, Pallas kernels, on_device(): pl.pallas_call(functools.partial(exchange_kernel, gx_n, gy_n), out_shape=...  39.9 us
    pallas_call x1, Pallas kernels, on_device(): pl.pallas_call(finish_kernel, out_shape=[jax.ShapeDtypeStruct((slots, 8,...  3.55 us

profile of v2, /device:TPU:1, one launch (start us, length us, event | category | flops | bytes accessed | tf_op | source)
XLA Modules:
  0.0 44.1 jit_solution(1508109686920915487)
XLA Ops:
  0.6 39.9 %exchange.1 = (f32[128,8,2048]{2,1,0:T(8,128)S(1)}, f32[136,128]{1,0:T(8,128)S(1)}, f32[8,128]{1,0:T(8,128)S(1)}, f32[32,32,128]{2,1,0:T(8,128)S(1)}) custom-call(f32[32,32,128]{2,1,0:T(8,128)} %t_hbm.1, bf16[32,128]{1,0:T(8,128)(2,1)} %amb_hbm.1, bf16[32,128]{1,0:T(8,128)(2,1)} %light_hbm.1, s32[1,64]{1,0:T(1,128)} %bitcast.6, s32[1,64]{1,0:T(1,128)} %bitcast.7, ...), custom_call_target="tpu_custom_call" | custom-call | tf_op jit(solution)/shard_map/exchange/pallas_call | solution.py:729
  40.6 3.6 %finish.1 = (f32[128,8,2048]{2,1,0:T(8,128)}, f32[32,32,128]{2,1,0:T(8,128)}) custom-call(f32[128,8,2048]{2,1,0:T(8,128)S(1)} %get-tuple-element.8.pre_ref, f32[136,128]{1,0:T(8,128)S(1)} %get-tuple-element.9.cnt_ref, f32[8,128]{1,0:T(8,128)S(1)} %get-tuple-element.10.shift_ref, f32[32,32,128]{2,1,0:T(8,128)S(1)} %get-tuple-element.11.therm_ref), custom_call_target="tpu_custom_call" | custom-call | tf_op jit(solution)/shard_map/finish/pallas_call | solution.py:802

commit v3 on v2

--- a/solution.py
+++ b/solution.py
@@ -20,7 +20,6 @@
 
 LEVELS = 32
 BLOCKS = 64
-ROWS = 144
 UNROLL = 4
 LEVEL_STEP = 8
 OUT_STEP = 8
@@ -78,6 +77,9 @@
     step_ref,
     pay_ref,
     recv_ref,
+    ax_ref,
+    axr_ref,
+    top_ref,
     hs_ref,
     hr_ref,
     tmp_ref,
@@ -98,6 +100,8 @@
     c_sem,
     halo_s,
     halo_r,
+    xs_sem,
+    xr_sem,
     fs_sem,
     fr_sem,
     own_sem,
@@ -239,20 +243,6 @@
     for copy in halos:
         copy.start()
 
-    lane_n = iota((1, 512), 1)
-    key_l = slot_l * 8.0 + (lane_n & 7).astype(F32)
-
-    def build_sel(z, carry):
-        m = iota((256, 1), 0) + z * 256
-        key = ((m >> 6) << 6) | ((m & 7) << 3) | ((m >> 3) & 7)
-        sel_ref[pl.ds(pl.multiple_of(z * 256, 256), 256), :] = one_hot(
-            jnp.broadcast_to(key.astype(F32), (256, 512))
-            == jnp.broadcast_to(key_l, (256, 512))
-        )
-        return carry
-
-    lax.fori_loop(0, nz, build_sel, 0)
-
     def by_lanes(field):
         return jnp.concatenate([field[8 * bx : 8 * bx + 8] for bx in range(4)], axis=1)
 
@@ -278,9 +268,48 @@
     )
     packed_aux = lax.dot_general(sel_b, wide, NT, preferred_element_type=F32)
     packed_aux = packed_aux.reshape(gy_n, 8, 256)
-    pay_ref[:, 128:144, :] = jnp.concatenate(
+    ax_ref[...] = jnp.concatenate(
         [packed_aux[:, :, :128], packed_aux[:, :, 128:]], axis=1
     ).astype(BF16)
+
+    def aux_send(other):
+        return pltpu.make_async_remote_copy(
+            ax_ref.at[other],
+            axr_ref.at[my],
+            xs_sem.at[other],
+            xr_sem.at[my],
+            device_id={"gy": other},
+            device_id_type=MESH,
+        )
+
+    def aux_arrival(other):
+        return pltpu.make_async_remote_copy(
+            ax_ref.at[other],
+            axr_ref.at[other],
+            xs_sem.at[other],
+            xr_sem.at[other],
+            device_id={"gy": other},
+            device_id_type=MESH,
+        )
+
+    own_aux = pltpu.make_async_copy(ax_ref.at[my], axr_ref.at[my], own_sem.at[2])
+    own_aux.start()
+    for d in range(1, gy_n):
+        aux_send((my + d) % gy_n).start()
+
+    lane_n = iota((1, 512), 1)
+    key_l = slot_l * 8.0 + (lane_n & 7).astype(F32)
+
+    def build_sel(z, carry):
+        m = iota((256, 1), 0) + z * 256
+        key = ((m >> 6) << 6) | ((m & 7) << 3) | ((m >> 3) & 7)
+        sel_ref[pl.ds(pl.multiple_of(z * 256, 256), 256), :] = one_hot(
+            jnp.broadcast_to(key.astype(F32), (256, 512))
+            == jnp.broadcast_to(key_l, (256, 512))
+        )
+        return carry
+
+    lax.fori_loop(0, nz, build_sel, 0)
 
     for copy in halos:
         copy.wait_recv()
@@ -403,6 +432,7 @@
     ).astype(BF16)
     upper = lane >= 64
     upper8 = lane8 >= 64
+    level = jnp.where(upper, 1.0, 0.0)
     sums = (zero8,) * 4
 
     def back(other):
@@ -474,79 +504,41 @@
             gx_send((mx + d) % gx_n).start()
         ara_ref[mx] = ar_ref[0]
 
+    def row_of(ref, i, s):
+        return ref[i, pl.ds(s, 8, stride=0), :]
+
+    def mix_of(i, s):
+        return mix_ref[pl.ds(pl.multiple_of(s * 8, 8), 8), 128 * i : 128 * i + 128]
+
     for q in range(nz):
         z = (mz - q + nz) % nz
         s0 = z * 32
         for d in range(4):
             if q == 0 and d == 0:
-                own.wait()
+                own_aux.wait()
             else:
-                arrival(z * 4 + (mq - d + 4) % 4).wait_recv()
+                aux_arrival(z * 4 + (mq - d + 4) % 4).wait_recv()
         c_copy(z).wait()
-        blk = recv_ref[pl.ds(z * 4, 4), :, :].astype(F32)
-        rows = []
-        for h in range(2):
-            quads = []
-            for yh in range(2):
-                quads.append(
-                    swap_chunks(
-                        [
-                            blk[:, h * 64 + y * 8 : h * 64 + y * 8 + 8, :].reshape(32, 128)
-                            for y in range(yh * 4, yh * 4 + 4)
-                        ]
-                    )
-                )
-            for g in range(4):
-                rows.append(jnp.concatenate([quads[0][g], quads[1][g]], axis=1))
-        cols = jnp.dot(
-            jnp.concatenate(rows, axis=0).astype(BF16),
-            to_columns,
-            preferred_element_type=F32,
-        )
-        for g in range(8):
-            tmp_ref[:, g * 256 : g * 256 + 256] = cols[g * 32 : g * 32 + 32]
-
-        la = blk[:, 128:136, :].reshape(32, 128)
-        cnt = blk[:, 136:144, :].reshape(32, 128)
+        got = axr_ref[pl.ds(z * 4, 4), :, :].astype(F32)
+        la = got[:, 0:8, :].reshape(32, 128)
+        cnt = got[:, 8:16, :].reshape(32, 128)
         cnt_ref[pl.ds(s0, 32), :] = cnt
-        la_r = pltpu.roll(la, 64, 1)
-        light = jnp.where(upper, la_r, la)
-        amb = jnp.where(upper, la, la_r)
-        level = jnp.where(upper, 1.0, 0.0)
+        light = jnp.where(upper, pltpu.roll(la, 64, 1), la)
         run = jnp.zeros((32, 128), F32)
         prev = light
-        kap_prev = jnp.zeros((32, 128), F32)
-        t_next = tmp_ref[:, 0:128]
-        tr_next = pltpu.roll(t_next, 64, 1)
+        wet = cnt - level
         for i in range(16):
             at = slice(128 * i, 128 * i + 128)
-            t_i, tr_i = t_next, tr_next
-            if i < 15:
-                t_next = tmp_ref[:, 128 * i + 128 : 128 * i + 256]
-                tr_next = pltpu.roll(t_next, 64, 1)
-                t_below = jnp.where(upper, tr_next, tr_i)
-            else:
-                t_below = jnp.where(upper, t_i, tr_i)
             atten = ATTEN_WATER + ATTEN_CHL * c_ref[pl.ds(s0, 32), 0, at]
-            atten_r = pltpu.roll(atten, 64, 1)
-            both = atten + atten_r
+            both = atten + pltpu.roll(atten, 64, 1)
             cum = run + jnp.where(upper, both, atten)
             run = run + both
             bottom = light * jnp.exp(-cum)
             bottom_r = pltpu.roll(bottom, 64, 1)
             top = jnp.where(upper, bottom_r, prev)
             prev = bottom_r
-            wet = cnt - 2.0 * i > level
-            heat_ref[:, at] = jnp.where(wet, top - bottom, 0.0)
-            growth = jnp.exp(GROWTH_TEMP * t_i) * top / (top + 1.0)
-            gv_ref[i, 0:32] = jnp.where(wet, STEP_DT * growth, 0.0)
-            kap = amb * (1.0 + 0.5 * jnp.tanh(t_i - t_below))
-            kap = jnp.where(cnt - (2.0 * i + 1.0) > level, STEP_DT * kap, 0.0)
-            kap_r = pltpu.roll(kap, 64, 1)
-            kap_ref[i, 0:32] = kap
-            kup_ref[i, 0:32] = jnp.where(upper, kap_r, kap_prev)
-            kap_prev = kap_r
-
+            top_ref[i, pl.ds(s0, 32), :] = top
+            heat_ref[:, at] = jnp.where(wet > 2.0 * i, top - bottom, 0.0)
         heat = jnp.concatenate(
             [heat_ref[:, g * 256 : g * 256 + 256] for g in range(8)], axis=0
         ).astype(BF16)
@@ -568,72 +560,115 @@
                 hs_ref[pl.ds(z * 4, 4), h * 64 + y * 8 : h * 64 + y * 8 + 16, :] = (
                     jnp.concatenate([flat[y], flat[y + 1]], axis=1).astype(BF16)
                 )
+    for q in range(nz):
+        z = (mz - q + nz) % nz
+        s0 = z * 32
         for d in range(4):
             if q == 0 and d == 0:
-                own_back.start()
+                own.wait()
             else:
-                back(z * 4 + (mq - d + 4) % 4).start()
+                arrival(z * 4 + (mq - d + 4) % 4).wait_recv()
+        blk = recv_ref[pl.ds(z * 4, 4), :, :].astype(F32)
+        rows = []
+        for h in range(2):
+            quads = []
+            for yh in range(2):
+                quads.append(
+                    swap_chunks(
+                        [
+                            blk[:, h * 64 + y * 8 : h * 64 + y * 8 + 8, :].reshape(32, 128)
+                            for y in range(yh * 4, yh * 4 + 4)
+                        ]
+                    )
+                )
+            for g in range(4):
+                rows.append(jnp.concatenate([quads[0][g], quads[1][g]], axis=1))
+        cols = jnp.dot(
+            jnp.concatenate(rows, axis=0).astype(BF16),
+            to_columns,
+            preferred_element_type=F32,
+        )
+        for g in range(8):
+            tmp_ref[:, g * 256 : g * 256 + 256] = cols[g * 32 : g * 32 + 32]
+
+        got = axr_ref[pl.ds(z * 4, 4), :, :].astype(F32)
+        la = got[:, 0:8, :].reshape(32, 128)
+        cnt = got[:, 8:16, :].reshape(32, 128)
+        amb = jnp.where(upper, la, pltpu.roll(la, 64, 1))
+        wet = cnt - level
+        kap_prev = jnp.zeros((32, 128), F32)
+        t_next = tmp_ref[:, 0:128]
+        tr_next = pltpu.roll(t_next, 64, 1)
+        for i in range(16):
+            t_i, tr_i = t_next, tr_next
+            if i < 15:
+                t_next = tmp_ref[:, 128 * i + 128 : 128 * i + 256]
+                tr_next = pltpu.roll(t_next, 64, 1)
+                t_below = jnp.where(upper, tr_next, tr_i)
+            else:
+                t_below = jnp.where(upper, t_i, tr_i)
+            top = top_ref[i, pl.ds(s0, 32), :]
+            growth = jnp.exp(GROWTH_TEMP * t_i) * top / (top + 1.0)
+            gv_ref[i, pl.ds(s0, 32)] = jnp.where(wet > 2.0 * i, STEP_DT * growth, 0.0)
+            kap = amb * (1.0 + 0.5 * jnp.tanh(t_i - t_below))
+            kap = jnp.where(wet > 2.0 * i + 1.0, STEP_DT * kap, 0.0)
+            kap_r = pltpu.roll(kap, 64, 1)
+            kap_ref[i, pl.ds(s0, 32)] = kap
+            kup_ref[i, pl.ds(s0, 32)] = jnp.where(upper, kap_r, kap_prev)
+            kap_prev = kap_r
 
         for g in range(8):
             at = slice(256 * g, 256 * g + 256)
             c_b = c_ref[pl.ds(s0, 32), :, at].reshape(256, 256).astype(BF16)
-            mix_ref[:, at] = jnp.dot(mat_hi, c_b, preferred_element_type=F32) + jnp.dot(
+            mix_ref[pl.ds(pl.multiple_of(s0 * 8, 256), 256), at] = jnp.dot(mat_hi, c_b, preferred_element_type=F32) + jnp.dot(
                 mat_lo, c_b, preferred_element_type=F32
             )
-
-        def row_of(ref, i, s):
-            return ref[i, pl.ds(s, 8, stride=0), :]
-
-        def mix_of(i, s):
-            return mix_ref[
-                pl.ds(pl.multiple_of(s * 8, 8), 8), 128 * i : 128 * i + 128
-            ]
 
         def grow(step, acc):
             acc = list(acc)
             for u in range(UNROLL):
-                s = step * UNROLL + u
+                s = s0 + step * UNROLL + u
                 for i in range(16):
                     acc[i % 4] = acc[i % 4] + row_of(gv_ref, i, s) * mix_of(i, s)
             return tuple(acc)
 
-        def tracers(counted, step, acc):
-            acc = list(acc)
-            for u in range(UNROLL):
-                s = step * UNROLL + u
-                c_next = c_ref[s0 + s, :, 0:128]
-                cr_next = pltpu.roll(c_next, 64, 1)
-                cr_i = cr_next
-                for i in range(16):
-                    at = slice(128 * i, 128 * i + 128)
-                    cr_prev = cr_i
-                    c_i, cr_i = c_next, cr_next
-                    if i < 15:
-                        c_next = c_ref[s0 + s, :, 128 * i + 128 : 128 * i + 256]
-                        cr_next = pltpu.roll(c_next, 64, 1)
-                    below = jnp.where(upper8, cr_next, cr_i)
-                    above = jnp.where(upper8, cr_i, cr_prev)
-                    grown = row_of(gv_ref, i, s) * mix_of(i, s)
-                    if counted:
-                        acc[i % 4] = acc[i % 4] + grown
-                    pre_ref[s0 + s, :, at] = (c_i + row_of(kap_ref, i, s) * (below - c_i)) + (
-                        row_of(kup_ref, i, s) * (above - c_i) + grown
-                    )
-            return tuple(acc)
-
-        last = q == nz - 1
-        steps = 32 // UNROLL
-        if last:
-            sums = lax.fori_loop(0, steps, grow, sums)
-            gx_sums(sums)
-        sums = lax.fori_loop(0, steps, functools.partial(tracers, not last), sums)
-
+        sums = lax.fori_loop(0, 32 // UNROLL, grow, sums)
+    gx_sums(sums)
+
+    own_back.start()
+    for d in range(1, gy_n):
+        back((my + d) % gy_n).start()
+
+    def tracers(step, carry):
+        for u in range(UNROLL):
+            s = step * UNROLL + u
+            c_next = c_ref[s, :, 0:128]
+            cr_next = pltpu.roll(c_next, 64, 1)
+            cr_i = cr_next
+            for i in range(16):
+                at = slice(128 * i, 128 * i + 128)
+                cr_prev = cr_i
+                c_i, cr_i = c_next, cr_next
+                if i < 15:
+                    c_next = c_ref[s, :, 128 * i + 128 : 128 * i + 256]
+                    cr_next = pltpu.roll(c_next, 64, 1)
+                below = jnp.where(upper8, cr_next, cr_i)
+                above = jnp.where(upper8, cr_i, cr_prev)
+                grown = row_of(gv_ref, i, s) * mix_of(i, s)
+                pre_ref[s, :, at] = (c_i + row_of(kap_ref, i, s) * (below - c_i)) + (
+                    row_of(kup_ref, i, s) * (above - c_i) + grown
+                )
+        return carry
+
+    steps = slots // UNROLL
+    lax.fori_loop(0, steps // 2, tracers, 0)
     for d in range(1, gx_n):
         gx_arrival((mx + d) % gx_n).wait_recv()
     ar_ref[1] = jnp.sum(ara_ref[...], axis=0)
     for d in range(1, gy_n):
         gy_send((my + d) % gy_n).start()
     arb_ref[my] = ar_ref[1]
+    lax.fori_loop(steps // 2, steps, tracers, 0)
 
     for q in range(nz):
         z = (mz + q) % nz
@@ -664,20 +699,23 @@
 
     lax.fori_loop(0, LEVELS, finish, 0)
 
+    for copy in halos:
+        copy.wait_send()
+    for d in range(1, gy_n):
+        forward((my + d) % gy_n).wait_send()
+        back((my + d) % gy_n).wait_send()
+        aux_send((my + d) % gy_n).wait_send()
+    for d in range(1, gx_n):
+        gx_send((mx + d) % gx_n).wait_send()
+
     for d in range(1, gy_n):
         gy_arrival((my + d) % gy_n).wait_recv()
     total = jnp.sum(arb_ref[...], axis=0)
     grown = jnp.sum(total[0:8], axis=1, keepdims=True)
     shift_ref[...] = -(jnp.broadcast_to(grown, (8, 128)) / jnp.maximum(total[8:16], 1.0))
 
-    for copy in halos:
-        copy.wait_send()
     for d in range(1, gy_n):
-        forward((my + d) % gy_n).wait_send()
-        back((my + d) % gy_n).wait_send()
         gy_send((my + d) % gy_n).wait_send()
-    for d in range(1, gx_n):
-        gx_send((mx + d) % gx_n).wait_send()
 
 
 def finish_kernel(pre_ref, cnt_ref, shift_ref, therm_ref, out_ref, thout_ref, buf_ref, sem):
@@ -748,16 +786,19 @@
                 pltpu.VMEM((64 * gy_n, 512), BF16),
                 pltpu.VMEM((256, 512), BF16),
                 pltpu.VMEM((32, 32, 128), F32),
-                pltpu.VMEM((gy_n, ROWS, 128), BF16),
-                pltpu.VMEM((gy_n, ROWS, 128), BF16),
+                pltpu.VMEM((gy_n, 128, 128), BF16),
+                pltpu.VMEM((gy_n, 128, 128), BF16),
+                pltpu.VMEM((gy_n, 16, 128), BF16),
+                pltpu.VMEM((gy_n, 16, 128), BF16),
+                pltpu.VMEM((16, slots, 128), F32),
                 pltpu.VMEM((gy_n, 128, 128), BF16),
                 pltpu.VMEM((gy_n, 128, 128), BF16),
                 pltpu.VMEM((32, 2048), F32),
                 pltpu.VMEM((32, 2048), F32),
-                pltpu.VMEM((16, 40, 128), F32),
-                pltpu.VMEM((16, 40, 128), F32),
-                pltpu.VMEM((16, 40, 128), F32),
-                pltpu.VMEM((256, 2048), F32),
+                pltpu.VMEM((16, slots + 8, 128), F32),
+                pltpu.VMEM((16, slots + 8, 128), F32),
+                pltpu.VMEM((16, slots + 8, 128), F32),
+                pltpu.VMEM((8 * slots, 2048), F32),
                 pltpu.VMEM((256, 512), F32),
                 pltpu.VMEM((2, 40, 128), F32),
                 pltpu.VMEM((2, 40, 128), F32),
@@ -772,7 +813,9 @@
                 dma((4,)),
                 dma((gy_n,)),
                 dma((gy_n,)),
-                dma((2,)),
+                dma((gy_n,)),
+                dma((gy_n,)),
+                dma((3,)),
                 dma((gy_n,)),
                 dma((gy_n,)),
                 dma((gx_n,)),

time: 44.2 us -> 40.5 us (0.916)
  Pallas kernels: 43.5 us -> 39.7 us
    pallas_call x1, Pallas kernels: 39.9 us -> 36.2 us  [on_device(): pl.pallas_call(functools.partial(exchange_kernel, gx_n, gy_n), out_shape=...]
where the time goes in v3:
time: 40.5 us; the launch traced here: 40.4 us
  Pallas kernels  39.7 us (98%)
  between operations  0.64 us (2%)
    pallas_call x1, Pallas kernels, on_device(): pl.pallas_call(functools.partial(exchange_kernel, gx_n, gy_n), out_shape=...  36.2 us
    pallas_call x1, Pallas kernels, on_device(): pl.pallas_call(finish_kernel, out_shape=[jax.ShapeDtypeStruct((slots, 8,...  3.55 us

profile of v3, /device:TPU:1, one launch (start us, length us, event | category | flops | bytes accessed | tf_op | source)
XLA Modules:
  0.0 40.4 jit_solution(858300404169532796)
XLA Ops:
  0.6 36.2 %exchange.1 = (f32[128,8,2048]{2,1,0:T(8,128)S(1)}, f32[136,128]{1,0:T(8,128)S(1)}, f32[8,128]{1,0:T(8,128)S(1)}, f32[32,32,128]{2,1,0:T(8,128)S(1)}) custom-call(f32[32,32,128]{2,1,0:T(8,128)} %t_hbm.1, bf16[32,128]{1,0:T(8,128)(2,1)} %amb_hbm.1, bf16[32,128]{1,0:T(8,128)(2,1)} %light_hbm.1, s32[1,64]{1,0:T(1,128)} %bitcast.6, s32[1,64]{1,0:T(1,128)} %bitcast.7, ...), custom_call_target="tpu_custom_call" | custom-call | tf_op jit(solution)/shard_map/exchange/pallas_call | solution.py:767
  36.8 3.6 %finish.1 = (f32[128,8,2048]{2,1,0:T(8,128)}, f32[32,32,128]{2,1,0:T(8,128)}) custom-call(f32[128,8,2048]{2,1,0:T(8,128)S(1)} %get-tuple-element.8.pre_ref, f32[136,128]{1,0:T(8,128)S(1)} %get-tuple-element.9.cnt_ref, f32[8,128]{1,0:T(8,128)S(1)} %get-tuple-element.10.shift_ref, f32[32,32,128]{2,1,0:T(8,128)S(1)} %get-tuple-element.11.therm_ref), custom_call_target="tpu_custom_call" | custom-call | tf_op jit(solution)/shard_map/finish/pallas_call | solution.py:845

commit v4 on v3

--- a/solution.py
+++ b/solution.py
@@ -539,6 +539,13 @@
             prev = bottom_r
             top_ref[i, pl.ds(s0, 32), :] = top
             heat_ref[:, at] = jnp.where(wet > 2.0 * i, top - bottom, 0.0)
+        for g in range(8):
+            at = slice(256 * g, 256 * g + 256)
+            c_b = c_ref[pl.ds(s0, 32), :, at].reshape(256, 256).astype(BF16)
+            mix_ref[pl.ds(pl.multiple_of(s0 * 8, 256), 256), at] = jnp.dot(mat_hi, c_b, preferred_element_type=F32) + jnp.dot(
+                mat_lo, c_b, preferred_element_type=F32
+            )
+
         heat = jnp.concatenate(
             [heat_ref[:, g * 256 : g * 256 + 256] for g in range(8)], axis=0
         ).astype(BF16)
@@ -589,40 +596,14 @@
             preferred_element_type=F32,
         )
         for g in range(8):
-            tmp_ref[:, g * 256 : g * 256 + 256] = cols[g * 32 : g * 32 + 32]
-
-        got = axr_ref[pl.ds(z * 4, 4), :, :].astype(F32)
-        la = got[:, 0:8, :].reshape(32, 128)
-        cnt = got[:, 8:16, :].reshape(32, 128)
-        amb = jnp.where(upper, la, pltpu.roll(la, 64, 1))
-        wet = cnt - level
-        kap_prev = jnp.zeros((32, 128), F32)
-        t_next = tmp_ref[:, 0:128]
-        tr_next = pltpu.roll(t_next, 64, 1)
+            tmp_ref[pl.ds(s0, 32), g * 256 : g * 256 + 256] = cols[g * 32 : g * 32 + 32]
+
+        wet = cnt_ref[pl.ds(s0, 32), :] - level
         for i in range(16):
-            t_i, tr_i = t_next, tr_next
-            if i < 15:
-                t_next = tmp_ref[:, 128 * i + 128 : 128 * i + 256]
-                tr_next = pltpu.roll(t_next, 64, 1)
-                t_below = jnp.where(upper, tr_next, tr_i)
-            else:
-                t_below = jnp.where(upper, t_i, tr_i)
+            at = slice(128 * i, 128 * i + 128)
             top = top_ref[i, pl.ds(s0, 32), :]
-            growth = jnp.exp(GROWTH_TEMP * t_i) * top / (top + 1.0)
+            growth = jnp.exp(GROWTH_TEMP * tmp_ref[pl.ds(s0, 32), at]) * top / (top + 1.0)
             gv_ref[i, pl.ds(s0, 32)] = jnp.where(wet > 2.0 * i, STEP_DT * growth, 0.0)
-            kap = amb * (1.0 + 0.5 * jnp.tanh(t_i - t_below))
-            kap = jnp.where(wet > 2.0 * i + 1.0, STEP_DT * kap, 0.0)
-            kap_r = pltpu.roll(kap, 64, 1)
-            kap_ref[i, pl.ds(s0, 32)] = kap
-            kup_ref[i, pl.ds(s0, 32)] = jnp.where(upper, kap_r, kap_prev)
-            kap_prev = kap_r
-
-        for g in range(8):
-            at = slice(256 * g, 256 * g + 256)
-            c_b = c_ref[pl.ds(s0, 32), :, at].reshape(256, 256).astype(BF16)
-            mix_ref[pl.ds(pl.multiple_of(s0 * 8, 256), 256), at] = jnp.dot(mat_hi, c_b, preferred_element_type=F32) + jnp.dot(
-                mat_lo, c_b, preferred_element_type=F32
-            )
 
         def grow(step, acc):
             acc = list(acc)
@@ -638,6 +619,32 @@
     own_back.start()
     for d in range(1, gy_n):
         back((my + d) % gy_n).start()
+
+    def diffusion(z):
+        s0 = z * 32
+        la = axr_ref[pl.ds(z * 4, 4), 0:8, :].astype(F32).reshape(32, 128)
+        amb = jnp.where(upper, la, pltpu.roll(la, 64, 1))
+        wet = cnt_ref[pl.ds(s0, 32), :] - level
+        kap_prev = jnp.zeros((32, 128), F32)
+        t_next = tmp_ref[pl.ds(s0, 32), 0:128]
+        tr_next = pltpu.roll(t_next, 64, 1)
+        for i in range(16):
+            t_i, tr_i = t_next, tr_next
+            if i < 15:
+                t_next = tmp_ref[pl.ds(s0, 32), 128 * i + 128 : 128 * i + 256]
+                tr_next = pltpu.roll(t_next, 64, 1)
+                t_below = jnp.where(upper, tr_next, tr_i)
+            else:
+                t_below = jnp.where(upper, t_i, tr_i)
+            kap = amb * (1.0 + 0.5 * jnp.tanh(t_i - t_below))
+            kap = jnp.where(wet > 2.0 * i + 1.0, STEP_DT * kap, 0.0)
+            kap_r = pltpu.roll(kap, 64, 1)
+            kap_ref[i, pl.ds(s0, 32)] = kap
+            kup_ref[i, pl.ds(s0, 32)] = jnp.where(upper, kap_r, kap_prev)
+            kap_prev = kap_r
+
+    for z in range(nz):
+        diffusion(z)
 
     def tracers(step, carry):
         for u in range(UNROLL):
@@ -661,14 +668,14 @@
         return carry
 
     steps = slots // UNROLL
-    lax.fori_loop(0, steps // 2, tracers, 0)
+    lax.fori_loop(0, steps // 4, tracers, 0)
     for d in range(1, gx_n):
         gx_arrival((mx + d) % gx_n).wait_recv()
     ar_ref[1] = jnp.sum(ara_ref[...], axis=0)
     for d in range(1, gy_n):
         gy_send((my + d) % gy_n).start()
     arb_ref[my] = ar_ref[1]
-    lax.fori_loop(steps // 2, steps, tracers, 0)
+    lax.fori_loop(steps // 4, steps, tracers, 0)
 
     for q in range(nz):
         z = (mz + q) % nz
@@ -793,7 +800,7 @@
                 pltpu.VMEM((16, slots, 128), F32),
                 pltpu.VMEM((gy_n, 128, 128), BF16),
                 pltpu.VMEM((gy_n, 128, 128), BF16),
-                pltpu.VMEM((32, 2048), F32),
+                pltpu.VMEM((slots, 2048), F32),
                 pltpu.VMEM((32, 2048), F32),
                 pltpu.VMEM((16, slots + 8, 128), F32),
                 pltpu.VMEM((16, slots + 8, 128), F32),

time: 40.5 us -> 39.7 us (0.980)
  Pallas kernels: 39.7 us -> 39 us
    pallas_call x1, Pallas kernels: 36.2 us -> 35.4 us  [on_device(): pl.pallas_call(functools.partial(exchange_kernel, gx_n, gy_n), out_shape=...]
where the time goes in v4:
time: 39.7 us; the launch traced here: 39.6 us
  Pallas kernels  39 us (98%)
  between operations  0.64 us (2%)
    pallas_call x1, Pallas kernels, on_device(): pl.pallas_call(functools.partial(exchange_kernel, gx_n, gy_n), out_shape=...  35.4 us
    pallas_call x1, Pallas kernels, on_device(): pl.pallas_call(finish_kernel, out_shape=[jax.ShapeDtypeStruct((slots, 8,...  3.55 us

profile of v4, /device:TPU:1, one launch (start us, length us, event | category | flops | bytes accessed | tf_op | source)
XLA Modules:
  0.0 39.6 jit_solution(1146188466425516526)
XLA Ops:
  0.6 35.4 %exchange.1 = (f32[128,8,2048]{2,1,0:T(8,128)S(1)}, f32[136,128]{1,0:T(8,128)S(1)}, f32[8,128]{1,0:T(8,128)S(1)}, f32[32,32,128]{2,1,0:T(8,128)S(1)}) custom-call(f32[32,32,128]{2,1,0:T(8,128)} %t_hbm.1, bf16[32,128]{1,0:T(8,128)(2,1)} %amb_hbm.1, bf16[32,128]{1,0:T(8,128)(2,1)} %light_hbm.1, s32[1,64]{1,0:T(1,128)} %bitcast.6, s32[1,64]{1,0:T(1,128)} %bitcast.7, ...), custom_call_target="tpu_custom_call" | custom-call | tf_op jit(solution)/shard_map/exchange/pallas_call | solution.py:774
  36.1 3.6 %finish.1 = (f32[128,8,2048]{2,1,0:T(8,128)}, f32[32,32,128]{2,1,0:T(8,128)}) custom-call(f32[128,8,2048]{2,1,0:T(8,128)S(1)} %get-tuple-element.8.pre_ref, f32[136,128]{1,0:T(8,128)S(1)} %get-tuple-element.9.cnt_ref, f32[8,128]{1,0:T(8,128)S(1)} %get-tuple-element.10.shift_ref, f32[32,32,128]{2,1,0:T(8,128)S(1)} %get-tuple-element.11.therm_ref), custom_call_target="tpu_custom_call" | custom-call | tf_op jit(solution)/shard_map/finish/pallas_call | solution.py:852

commit v5 on v4

--- a/solution.py
+++ b/solution.py
@@ -373,46 +373,46 @@
             ).astype(BF16)
         return low_h, high_h
 
-    lax.fori_loop(
-        0, LEVELS // LEVEL_STEP, stencil, (hyr_ref[0, 0:8, :], hyr_ref[1, 0:8, :]))
-
-    def forward(other):
-        return pltpu.make_async_remote_copy(
-            pay_ref.at[other],
-            recv_ref.at[my],
-            fs_sem.at[other],
-            fr_sem.at[my],
+    def forward(other, h):
+        rows = pl.ds(h * 64, 64)
+        return pltpu.make_async_remote_copy(
+            pay_ref.at[other, rows],
+            recv_ref.at[my, rows],
+            fs_sem.at[h, other],
+            fr_sem.at[h, my],
             device_id={"gy": other},
             device_id_type=MESH,
         )
 
-    def arrival(other):
-        return pltpu.make_async_remote_copy(
-            pay_ref.at[other],
-            recv_ref.at[other],
-            fs_sem.at[other],
-            fr_sem.at[other],
+    def arrival(other, h):
+        rows = pl.ds(h * 64, 64)
+        return pltpu.make_async_remote_copy(
+            pay_ref.at[other, rows],
+            recv_ref.at[other, rows],
+            fs_sem.at[h, other],
+            fr_sem.at[h, other],
             device_id={"gy": other},
             device_id_type=MESH,
         )
 
     own = pltpu.make_async_copy(pay_ref.at[my], recv_ref.at[my], own_sem.at[0])
-    for q in range(nz):
-        z = (mz + q) % nz
-        part = lax.dot_general(
-            sel_ref[pl.ds(pl.multiple_of(z * 256, 256), 256), :],
-            ut_ref[...],
-            NT,
-            preferred_element_type=F32,
-        ).astype(BF16)
-        part = part.reshape(4, 64, 256)
-        pay_ref[pl.ds(z * 4, 4), 0:64, :] = part[:, :, :128]
-        pay_ref[pl.ds(z * 4, 4), 64:128, :] = part[:, :, 128:]
-        for d in range(4):
-            if q == 0 and d == 0:
-                own.start()
-            else:
-                forward(z * 4 + (mq + d) % 4).start()
+    edges = (hyr_ref[0, 0:8, :], hyr_ref[1, 0:8, :])
+    half_steps = LEVELS // LEVEL_STEP // 2
+    for h in range(2):
+        edges = lax.fori_loop(h * half_steps, (h + 1) * half_steps, stencil, edges)
+        for q in range(nz):
+            z = (mz + q) % nz
+            part = lax.dot_general(
+                sel_ref[pl.ds(pl.multiple_of(z * 256, 256), 256), :],
+                ut_ref[h * 128 : h * 128 + 128, :],
+                NT,
+                preferred_element_type=F32,
+            ).astype(BF16)
+            pay_ref[pl.ds(z * 4, 4), h * 64 : h * 64 + 64, :] = part.reshape(4, 64, 128)
+            for d in range(4):
+                if q or d:
+                    forward(z * 4 + (mq + d) % 4, h).start()
+    own.start()
 
     pi = iota((256, 256), 0)
     po = iota((256, 256), 1)
@@ -574,7 +574,8 @@
             if q == 0 and d == 0:
                 own.wait()
             else:
-                arrival(z * 4 + (mq - d + 4) % 4).wait_recv()
+                arrival(z * 4 + (mq - d + 4) % 4, 0).wait_recv()
+                arrival(z * 4 + (mq - d + 4) % 4, 1).wait_recv()
         blk = recv_ref[pl.ds(z * 4, 4), :, :].astype(F32)
         rows = []
         for h in range(2):
@@ -709,7 +710,8 @@
     for copy in halos:
         copy.wait_send()
     for d in range(1, gy_n):
-        forward((my + d) % gy_n).wait_send()
+        forward((my + d) % gy_n, 0).wait_send()
+        forward((my + d) % gy_n, 1).wait_send()
         back((my + d) % gy_n).wait_send()
         aux_send((my + d) % gy_n).wait_send()
     for d in range(1, gx_n):
@@ -820,8 +822,8 @@
                 dma((4,)),
                 dma((gy_n,)),
                 dma((gy_n,)),
-                dma((gy_n,)),
-                dma((gy_n,)),
+                dma((2, gy_n)),
+                dma((2, gy_n)),
                 dma((3,)),
                 dma((gy_n,)),
                 dma((gy_n,)),

time: 39.7 us -> 39.4 us (level)
  no operation moved by 1% of the time
where the time goes in v5:
time: 39.4 us; the launch traced here: 39.3 us
  Pallas kernels  38.7 us (98%)
  between operations  0.64 us (2%)
    pallas_call x1, Pallas kernels, on_device(): pl.pallas_call(functools.partial(exchange_kernel, gx_n, gy_n), out_shape=...  35.1 us
    pallas_call x1, Pallas kernels, on_device(): pl.pallas_call(finish_kernel, out_shape=[jax.ShapeDtypeStruct((slots, 8,...  3.55 us

profile of v5, /device:TPU:1, one launch (start us, length us, event | category | flops | bytes accessed | tf_op | source)
XLA Modules:
  0.0 39.3 jit_solution(11975142161740369298)
XLA Ops:
  0.6 35.1 %exchange.1 = (f32[128,8,2048]{2,1,0:T(8,128)S(1)}, f32[136,128]{1,0:T(8,128)S(1)}, f32[8,128]{1,0:T(8,128)S(1)}, f32[32,32,128]{2,1,0:T(8,128)S(1)}) custom-call(f32[32,32,128]{2,1,0:T(8,128)} %t_hbm.1, bf16[32,128]{1,0:T(8,128)(2,1)} %amb_hbm.1, bf16[32,128]{1,0:T(8,128)(2,1)} %light_hbm.1, s32[1,64]{1,0:T(1,128)} %bitcast.6, s32[1,64]{1,0:T(1,128)} %bitcast.7, ...), custom_call_target="tpu_custom_call" | custom-call | tf_op jit(solution)/shard_map/exchange/pallas_call | solution.py:776
  35.8 3.6 %finish.1 = (f32[128,8,2048]{2,1,0:T(8,128)}, f32[32,32,128]{2,1,0:T(8,128)}) custom-call(f32[128,8,2048]{2,1,0:T(8,128)S(1)} %get-tuple-element.8.pre_ref, f32[136,128]{1,0:T(8,128)S(1)} %get-tuple-element.9.cnt_ref, f32[8,128]{1,0:T(8,128)S(1)} %get-tuple-element.10.shift_ref, f32[32,32,128]{2,1,0:T(8,128)S(1)} %get-tuple-element.11.therm_ref), custom_call_target="tpu_custom_call" | custom-call | tf_op jit(solution)/shard_map/finish/pallas_call | solution.py:854
